TPU v7x, 512 devices: a whole 4x4x16 slice. The times are simulated.
512 devices in a mesh: tm: 128 (over z, x, y_lo), tile: 4 (over y_hi, core).
Axes of the slice: x: 4, y: 4 (y_hi: 2, y_lo: 2; y = y_hi * 2 + y_lo), z: 16, core: 2. Of those that a mesh axis runs over, the one named last changes fastest.
Arguments:
- operator: float32 [128, 768, 768], P('tm', 'tile'), may hold values from -4 to 20, as said below
- initial: float32 [128, 768, 768], P('tm', 'tile'), may hold values from -1 to 2, as said below
- block_sizes: int32 [128], P('tm'), may hold values from 512 to 768, as said below
- link_index: int32 [128, 512], P('tm'), may hold values from 0 to 511, as said below
- link_pair: bfloat16 [128, 768, 512], P('tm', 'tile'), may hold values from -0.4375 to 0.4375
- link_global: bfloat16 [128, 768, 512], P('tm', 'tile'), may hold values from -0.109375 to 0.109375
- schur_base: float32 [512, 512], P('tile'), may hold values from -4 to 20, as said below
- schur_start: float32 [512, 512], P('tile'), may hold values from -1 to 2, as said below
Outputs:
- link_diag: float32 [128, 256, 256], P('tm', 'tile')
- link_off: float32 [128, 256, 256], P('tm', 'tile')
- link_cross: float32 [128, 256, 512], P('tm', 'tile')
- global_schur: float32 [512, 512], P('tile')
- back_cols: float32 [128, 768, 512], P('tm', 'tile')
Inputs may be any that keep to these rules, and one draw needn't show every extreme that they name: `operator`: symmetric. `initial`: symmetric. `schur_base`: symmetric. `schur_start`: symmetric. `block_sizes`: some block has 768 live variables and some has 512. `link_index`: each row is a permutation of 0 to 511 that keeps every index j within its group of 128, j // 128.
All inputs are finite; a program needn't handle non-finite values.
Results may differ from a plain program's by a relative error of at most 0.0003.
Values may be sent and summed in bfloat16 or wider, within the bound.
A program may use at most 64 MiB of HBM per device.

v0:
```python
import jax
import jax.numpy as jnp
from jax import lax
from jax.sharding import PartitionSpec as P

STEPS = 2


HIGH = lax.Precision.HIGHEST


def shifted_2(value, axis, by):
    size = lax.axis_size(axis)
    pairs = [(i, i + by) for i in range(size) if 0 <= i + by < size]
    return lax.ppermute(value, axis, pairs)


def batched(left_side, right_side):
    return jnp.einsum("bij,bjk->bik", left_side, right_side, precision=HIGH)


def fold_rows(left_side, piece):
    return batched(left_side, piece.astype(jnp.float32))


def fold_plain(left_side, piece):
    return jnp.dot(left_side, piece, precision=HIGH, preferred_element_type=jnp.float32)


def fold_blocks(left_side, piece):
    return jnp.einsum("bij,jk->bik", left_side, piece, precision=HIGH)


def place_terms(own_terms, next_terms, link_width):
    return jnp.concatenate(
        [
            own_terms[:, :, :link_width] + next_terms[:, :, :link_width],
            own_terms[:, :, link_width : 2 * link_width],
            own_terms[:, :, 2 * link_width :] + next_terms[:, :, link_width:],
        ],
        axis=2,
    )


def shards(
    operator, initial, block_sizes, link_index, link_pair, link_global, schur_base, schur_start
):
    tile_count = lax.axis_size("tile")
    tile_part = lax.axis_index("tile")
    block_count, row_count, block_order = operator.shape
    link_width = link_pair.shape[2] // 2
    global_width = link_global.shape[2]
    owner_rows = global_width // tile_count
    row_ids = tile_part * row_count + lax.iota(jnp.int32, row_count)
    col_ids = lax.iota(jnp.int32, block_order)
    row_live = (row_ids[None, :] < block_sizes[:, None]).astype(jnp.float32)
    col_live = (col_ids[None, :] < block_sizes[:, None]).astype(jnp.float32)
    unit_rows = (row_ids[:, None] == col_ids[None, :]).astype(jnp.float32)

    def effective(matrix):
        return (
            matrix * row_live[:, :, None] * col_live[:, None, :]
            + unit_rows[None] * (1.0 - row_live)[:, :, None]
        )

    k_rows = effective(operator)
    x_rows = effective(initial)
    k_whole = lax.all_gather(k_rows, "tile", axis=1, tiled=True)
    for step in range(STEPS):
        left_side = batched(x_rows, k_whole)
        product = fold_rows(left_side, lax.all_gather(x_rows, "tile", axis=1, tiled=True))
        x_rows = 2.0 * x_rows - product
    live_half = row_live[:, :, None].astype(jnp.bfloat16)
    pair_live = link_pair * live_half
    glob_live = jnp.take_along_axis(link_global, link_index[:, None, :], axis=2) * live_half
    links_rows = jnp.concatenate([pair_live, glob_live], axis=2)
    solved = fold_rows(x_rows, lax.all_gather(links_rows, "tile", axis=1, tiled=True))
    own_links = links_rows.astype(jnp.float32)
    e_rows = own_links[:, :, :link_width]
    f_rows = own_links[:, :, link_width : 2 * link_width]
    g_rows = own_links[:, :, 2 * link_width :]
    y_e = solved[:, :, :link_width]
    y_f = solved[:, :, link_width : 2 * link_width]
    y_g = solved[:, :, 2 * link_width :]

    def inner(left_side, right_side):
        return jnp.einsum("bri,brj->bij", left_side, right_side, precision=HIGH)

    own_terms = jnp.concatenate(
        [inner(f_rows, y_f), inner(e_rows, y_f), inner(f_rows, y_g)], axis=2
    )
    next_terms = jnp.concatenate([inner(e_rows, y_e), inner(e_rows, y_g)], axis=2)
    global_terms = jnp.einsum("bri,brj->ij", g_rows, y_g, precision=HIGH)
    came = shifted_2(next_terms, "tm", -1)
    shifted = jnp.concatenate([next_terms[1:], came], axis=0)
    summed = lax.psum_scatter(
        place_terms(own_terms, shifted, link_width), "tile", scatter_dimension=1, tiled=True
    )
    totals = lax.psum(global_terms, ("tm", "tile"))
    panel = lax.dynamic_slice_in_dim(totals, tile_part * owner_rows, owner_rows, 0)
    global_schur = schur_base + panel
    first = fold_plain(schur_start, lax.all_gather(global_schur, "tile", axis=0, tiled=True))
    second = fold_plain(first, lax.all_gather(schur_start, "tile", axis=0, tiled=True))
    inverse_rows = 2.0 * schur_start - second
    back_cols = fold_blocks(y_g, lax.all_gather(inverse_rows, "tile", axis=0, tiled=True))
    link_diag = summed[:, :, :link_width]
    link_off = summed[:, :, link_width : 2 * link_width]
    link_cross = summed[:, :, 2 * link_width :]
    return (link_diag, link_off, link_cross, global_schur, back_cols)


def solution(mesh):
    return jax.shard_map(
        shards,
        mesh=mesh,
        in_specs=(
            P("tm", "tile", None),
            P("tm", "tile", None),
            P("tm"),
            P("tm", None),
            P("tm", "tile", None),
            P("tm", "tile", None),
            P("tile", None),
            P("tile", None),
        ),
        out_specs=(
            P("tm", "tile", None),
            P("tm", "tile", None),
            P("tm", "tile", None),
            P("tile", None),
            P("tm", "tile", None),
        ),
        check_vma=False,
    )
```

profile of v0, /device:TPU:1, one launch (start us, length us, event | category | flops | bytes accessed | tf_op | source)
XLA Modules:
  0.0 807.3 jit_solution(14458092901404295634)
XLA Ops:
  7.9 2.5 select_add_fusion.1
  10.5 0.7 all-gather.10.cloned.1.call-update
  11.3 40.8 %all-gather.8.cloned.1.call-done = f32[1,768,768]{2,1,0:T(8,128)} async-done(((f32[1,192,768]{2,1,0:T(8,128)}), f32[1,768,768]{2,1,0:T(8,128)}) %all-gather.8.cloned.1.call-update) | async-done | bytes 2359312 | tf_op jit(solution)/shard_map/all_gather | solution.py:68
  52.1 3.6 fusion.6
  55.7 33.8 %all-gather.10.cloned.1.call-done = f32[1,768,768]{2,1,0:T(8,128)} async-done(((f32[1,192,768]{2,1,0:T(8,128)}), f32[1,768,768]{2,1,0:T(8,128)}) %all-gather.10.cloned.1.call-update) | async-done | bytes 2359312 | tf_op jit(solution)/shard_map/all_gather | solution.py:71
  89.5 4.2 fusion.25
  94.0 0.8 copy.27
  94.8 2.6 gather_fusion
  97.4 1.2 broadcast_multiply_fusion
  98.6 0.9 pad_maximum_fusion.2
  99.5 2.0 copy.29
  101.6 2.5 fusion.4
  104.1 25.0 %all-gather.12.cloned.1.call-done = f32[1,768,768]{2,1,0:T(8,128)} async-done(((f32[1,192,768]{2,1,0:T(8,128)}), f32[1,768,768]{2,1,0:T(8,128)}) %all-gather.12.cloned.1.call-update) | async-done | bytes 2359312 | tf_op jit(solution)/shard_map/all_gather | solution.py:71
  129.2 3.6 fusion.22
  132.8 29.8 %all-gather.14.cloned.1.call-done = bf16[1,768,1024]{2,1,0:T(8,128)(2,1)} async-done(((bf16[1,192,1024]{2,1,0:T(8,128)(2,1)}), bf16[1,768,1024]{2,1,0:T(8,128)(2,1)}) %all-gather.14.cloned.1.call-update) | async-done | bytes 1572880 | tf_op jit(solution)/shard_map/all_gather | solution.py:77
  162.6 2.5 fusion.10
  165.1 1.6 fusion.30
  166.8 474.1 %all-reduce.4.cloned.1.call-done = f32[512,512]{1,0:T(8,128)} async-done(((f32[512,512]{1,0:T(8,128)}), f32[512,512]{1,0:T(8,128)}) %all-reduce.4.cloned.1.call-update) | async-done | bytes 1048592 | tf_op jit(solution)/shard_map/psum | solution.py:99
  640.9 1.7 dynamic-slice_add_fusion
  644.5 1.5 collective-permute-start
  646.4 22.9 %collective-permute-done = f32[1,256,768]{1,2,0:T(8,128)S(1)} collective-permute-done((f32[1,256,768]{1,2,0:T(8,128)S(1)}, f32[1,256,768]{1,2,0:T(8,128)S(1)}, u32[]{:S(2)}, u32[]{:S(2)}) %collective-permute-start) | collective-permute-done | bytes 786464 | tf_op jit(solution)/shard_map/ppermute | solution.py:15
  670.6 2.0 copy.32
  672.6 3.8 all-gather.16.cloned.1.call-done
  676.4 3.0 fusion.41
  679.4 24.3 %all-gather.18.cloned.1.call-done = f32[512,512]{1,0:T(8,128)} async-done(((f32[128,512]{1,0:T(8,128)}), f32[512,512]{1,0:T(8,128)}) %all-gather.18.cloned.1.call-update) | async-done | bytes 1048592 | tf_op jit(solution)/shard_map/all_gather | solution.py:103
  703.6 2.7 convolution_subtract_fusion
  706.4 1.3 dynamic-slice
  708.3 58.6 %all-reduce.6.cloned.1.call-done = f32[1,256,1024]{2,0,1:T(1,128)} async-done(((f32[1,256,1024]{2,0,1:T(1,128)}), f32[1,256,1024]{2,0,1:T(1,128)}) %all-reduce.6.cloned.1.call-update) | async-done | bytes 1048592
  766.8 1.2 constant_dynamic-slice_fusion.2
  768.8 1.1 constant_dynamic-slice_fusion
  771.1 26.8 %all-gather.20.cloned.1.call-done = f32[512,512]{1,0:T(8,128)} async-done(((f32[128,512]{1,0:T(8,128)}), f32[512,512]{1,0:T(8,128)}) %all-gather.20.cloned.1.call-update) | async-done | bytes 1048592 | tf_op jit(solution)/shard_map/all_gather | solution.py:105
  797.9 2.8 convolution_bitcast_fusion.2
  (54 shorter events, 6.1 us)
Async XLA Ops:
  7.2 44.9 %all-gather.8.cloned.1.call-start = ((), (), s32[]{:S(2)}) async-start(), calls=%async_computation | async-start | bytes 2949120 | tf_op jit(solution)/shard_map/all_gather | solution.py:68
  10.4 79.0 %copy-start = (f32[1,192,768]{2,1,0:T(8,128)S(1)}, f32[1,192,768]{2,1,0:T(8,128)}, u32[]{:S(2)}) copy-start(f32[1,192,768]{2,1,0:T(8,128)} %get-tuple-element.22) | copy-start | bytes 1769476
  10.5 79.0 %all-gather.10.cloned.1.call-start = ((), (), s32[]{:S(2)}) async-start(), calls=%async_computation.1 | async-start | bytes 2949120 | tf_op jit(solution)/shard_map/all_gather | solution.py:71
  11.2 117.9 %all-gather.12.cloned.1.call-start = ((), (), s32[]{:S(2)}) async-start(), calls=%async_computation.2 | async-start | bytes 2949120 | tf_op jit(solution)/shard_map/all_gather | solution.py:71
  55.7 38.1 %copy-start.6 = (bf16[1,192,512]{2,1,0:T(8,128)(2,1)S(1)}, bf16[1,192,512]{2,1,0:T(8,128)(2,1)}, u32[]{:S(2)}) copy-start(bf16[1,192,512]{2,1,0:T(8,128)(2,1)} %param.13) | copy-start | bytes 589828
  55.7 38.3 %copy-start.7 = (bf16[1,192,512]{2,1,0:T(8,128)(2,1)S(1)}, bf16[1,192,512]{2,1,0:T(8,128)(2,1)}, u32[]{:S(2)}) copy-start(bf16[1,192,512]{2,1,0:T(8,128)(2,1)} %param.12) | copy-start | bytes 589828
  55.7 39.1 %copy-start.8 = (s32[1,512]{1,0:T(1,128)S(1)}, s32[1,512]{1,0:T(1,128)}, u32[]{:S(2)}) copy-start(s32[1,512]{1,0:T(1,128)} %param.11) | copy-start | bytes 6148
  93.7 68.8 %all-gather.14.cloned.1.call-start = ((), (), s32[]{:S(2)}) async-start(), calls=%async_computation.3 | async-start | bytes 1966080 | tf_op jit(solution)/shard_map/all_gather | solution.py:77
  94.8 6.7 copy-start.1
  94.8 6.7 copy-start.2
  101.5 539.3 %all-reduce.4.cloned.1.call-start = ((), (), s32[]{:S(2)}) async-start(), calls=%async_computation.4 | async-start | bytes 2097152 | tf_op jit(solution)/shard_map/psum | solution.py:99
  132.8 32.3 %copy-start.4 = (bf16[512,192]{1,0:T(8,128)(2,1)S(1)}, bf16[512,192]{1,0:T(8,128)(2,1)}, u32[]{:S(2)}) copy-start(bf16[512,192]{1,0:T(8,128)(2,1)} %gather_fusion) | copy-start | bytes 589828
  132.8 508.1 %copy-start.5 = (f32[128,512]{1,0:T(8,128)S(1)}, f32[128,512]{1,0:T(8,128)}, u32[]{:S(2)}) copy-start(f32[128,512]{1,0:T(8,128)} %param.14) | copy-start | bytes 786436
  166.7 509.6 %all-gather.16.cloned.1.call-start = ((), (), s32[]{:S(2)}) async-start(), calls=%async_computation.5 | async-start | bytes 1310720 | tf_op jit(solution)/shard_map/all_gather | solution.py:102
  642.6 61.1 %all-gather.18.cloned.1.call-start = ((), (), s32[]{:S(2)}) async-start(), calls=%async_computation.6 | async-start | bytes 1310720 | tf_op jit(solution)/shard_map/all_gather | solution.py:103
  643.3 123.5 %all-reduce.6.cloned.1.call-start = ((), (), s32[]{:S(2)}) async-start(), calls=%async_computation.8 | async-start | bytes 2097152
  644.5 24.8 %collective-permute-start = (f32[1,256,768]{1,2,0:T(8,128)S(1)}, f32[1,256,768]{1,2,0:T(8,128)S(1)}, u32[]{:S(2)}, u32[]{:S(2)}) collective-permute-start(f32[1,256,768]{1,2,0:T(8,128)S(1)} %pad_maximum_fusion.1), channel_id=1, source_target_pairs={{4,0},{8,4},{12,8},{16,12},{20,16},{24,20},{28,24},{32,28},{36,32}... | collective-permute-start | bytes 2359304 | tf_op jit(solution)/shard_map/ppermute | solution.py:15
  670.5 5.9 copy-start.3
  672.5 125.3 %all-gather.20.cloned.1.call-start = ((), (), s32[]{:S(2)}) async-start(), calls=%async_computation.7 | async-start | bytes 1310720 | tf_op jit(solution)/shard_map/all_gather | solution.py:105
Sparse Core Ops, SparseCore 0:
  10.6 41.4 all-gather.7
  54.2 35.2 all-gather.9
  93.9 35.2 all-gather.11
  131.7 30.8 all-gather.13
  167.9 472.9 all-reduce.3
  643.4 32.9 all-gather.15
  678.5 25.1 all-gather.17
  706.6 60.2 all-reduce.5
  769.5 28.2 all-gather.19
where the time goes:
time: 808 us; the launch traced here: 807 us
  waiting for transfers between devices  741 us (92%)
  matrix products  29.2 us (4%)
  between operations  15.4 us (2%)
  local copies, waits for them, and re-layouts  13.1 us (2%)
    psum x1, waiting for transfers between devices, shards(): totals = lax.psum(global_terms, ('tm', 'tile'))  474 us
    unnamed x10, waiting for transfers between devices  60.1 us
    all_gather x2, waiting for transfers between devices, shards(): lax.all_gather(x_rows, 'tile', axis=1, tiled=True)  58.8 us
    all_gather x1, waiting for transfers between devices, shards(): k_whole = lax.all_gather(k_rows, 'tile', axis=1, tiled=True)  40.8 us
    all_gather x1, waiting for transfers between devices, shards(): lax.all_gather(links_rows, 'tile', axis=1, tiled=True)  29.8 us
    all_gather x1, waiting for transfers between devices, shards(): lax.all_gather(inverse_rows, 'tile', axis=0, tiled=True)  26.8 us
    all_gather x1, waiting for transfers between devices, shards(): lax.all_gather(schur_start, 'tile', axis=0, tiled=True)  24.3 us
    ppermute x1, waiting for transfers between devices, shifted_2(): return lax.ppermute(value, axis, pairs)  22.9 us
  transfers between devices with their start and end apart: 10, of which 10 were waited for; matrix products, arithmetic and copies ran while one was open for 4% of the time, Pallas kernels for 0%

commit v1 on v0

v1 whole, which is shorter than its diff:
```python
import functools

import jax
import jax.numpy as jnp
from jax import lax
from jax.experimental import pallas as pl
from jax.experimental.pallas import tpu as pltpu
from jax.sharding import PartitionSpec as P

MESH = pl.DeviceIdType.MESH
BF = jnp.bfloat16
F32 = jnp.float32
PLANE = 8
HALF = 384
ROWS = 192


def al(value, step):
    return pl.multiple_of(value, step)


def dot(left, right):
    return jnp.dot(left, right, preferred_element_type=F32)


def dot_nt(left, right):
    return lax.dot_general(left, right, (((1,), (1,)), ((), ())), preferred_element_type=F32)


def split(value):
    high = value.astype(BF)
    return high, (value - high.astype(F32)).astype(BF)


def product(value, high, low):
    value_high, value_low = split(value)
    return dot(value_high, high) + dot(value_high, low) + dot(value_low, high)


def position():
    tm = lax.axis_index("tm")
    ti = lax.axis_index("tile")
    h = ti // 2
    return tm, ti, h, ti - 2 * h


def remote(src, dst, send, recv, device):
    return pltpu.make_async_remote_copy(
        src_ref=src, dst_ref=dst, send_sem=send, recv_sem=recv, device_id=device, device_id_type=MESH
    )


def greet(devices):
    barrier = pltpu.get_barrier_semaphore()
    for device in devices:
        pl.semaphore_signal(barrier, inc=1, device_id=device, device_id_type=MESH)


def place_ids(h, first, count, axis, shape):
    ids = lax.broadcasted_iota(jnp.int32, shape, axis) + first
    return jnp.where(ids < HALF, ids + h * HALF, ids - h * HALF)


def gather_kernel(
    sizes, k_hbm, x_hbm, g_hbm,
    xh, xl, kh, kl, g_out,
    rows_x, rows_k, diag_x, diag_k, rows_g,
    local_sem, send_sem, recv_sem,
):
    tm, ti, h, c = position()
    mate = (tm, ti + 1 - 2 * c)
    cross = (tm, lax.rem(ti + 2, 4))
    size = sizes[0]
    greet((mate, cross))
    pl.semaphore_wait(pltpu.get_barrier_semaphore(), 2)
    own = al(h * HALF, 128)
    oth = al(HALF - h * HALF, 128)
    slots = [0]

    def slot():
        slots[0] += 1
        return slots[0] - 1

    def copy(src, dst, device):
        at = slot()
        made = remote(src, dst, send_sem.at[at], recv_sem.at[at], device)
        made.start()
        return made

    def pieces(ref):
        return [
            ref.at[pl.ds(al(256 * c, 128), 128), pl.ds(al(256 * c, 128), 128)],
            ref.at[pl.ds(al(256 * c, 128), 128), pl.ds(al(128 - 128 * c, 128), 128)],
            ref.at[pl.ds(al(128 + 64 * c, 64), 64), pl.ds(128, 256)],
        ]

    def other_pieces(ref):
        return pieces(ref)

    def sources(hbm):
        return [
            hbm.at[pl.ds(al(64 * c, 64), 128), pl.ds(al(own + 256 * c, 128), 128)],
            hbm.at[pl.ds(al(64 * c, 64), 128), pl.ds(al(own + 128 - 128 * c, 128), 128)],
            hbm.at[pl.ds(al(128 - 128 * c, 64), 64), pl.ds(al(own + 128, 128), 256)],
        ]

    mine = pl.ds(al(ROWS * c, 64), ROWS)
    far = pl.ds(al(HALF + ROWS * c, 64), ROWS)
    cross_x = [copy(a, b, cross) for a, b in zip(sources(x_hbm), pieces(diag_x))]
    cross_k = [copy(a, b, cross) for a, b in zip(sources(k_hbm), pieces(diag_k))]
    cross_g = copy(g_hbm, rows_g.at[far], cross)

    def halves(hbm, rows):
        return [
            (hbm.at[:, pl.ds(own, HALF)], rows.at[mine, pl.ds(0, HALF)]),
            (hbm.at[:, pl.ds(oth, HALF)], rows.at[mine, pl.ds(HALF, HALF)]),
        ]

    mate_x = [copy(a, b, mate) for a, b in halves(x_hbm, rows_x)]
    mate_k = [copy(a, b, mate) for a, b in halves(k_hbm, rows_k)]
    mate_g = copy(g_hbm, rows_g.at[mine], mate)
    local = []
    for a, b in halves(x_hbm, rows_x) + halves(k_hbm, rows_k) + [(g_hbm, rows_g.at[mine])]:
        made = pltpu.make_async_copy(a, b, local_sem.at[len(local)])
        made.start()
        local.append(made)

    def effective(block, first_row, first_col):
        row = place_ids(h, first_row, 0, 0, block.shape)
        col = place_ids(h, first_col, 0, 1, block.shape)
        unit = jnp.where(row == col, 1.0, 0.0).astype(F32)
        return jnp.where((row < size) & (col < size), block, unit)

    def store(high, low, row, col, value):
        n, m = value.shape
        value_high, value_low = split(value)
        high[pl.ds(row, n), pl.ds(col, m)] = value_high
        low[pl.ds(row, n), pl.ds(col, m)] = value_low

    def own_rows(rows, high, low):
        for i in range(3):
            at = 128 * i
            store(high, low, at, 0, effective(rows[pl.ds(at, 128), pl.ds(0, HALF)], at, 0))
            block = effective(rows[pl.ds(at, 128), pl.ds(HALF, HALF)], at, HALF)
            store(high, low, at, HALF, block)
            store(high, low, HALF, at, block.T)

    def far_rows(diag, high, low):
        for i in range(3):
            j, k = (i + 1) % 3, (i + 2) % 3
            at = HALF + 128 * i
            for col, block in (
                (i, diag[pl.ds(128 * i, 128), pl.ds(128 * i, 128)]),
                (j, diag[pl.ds(128 * i, 128), pl.ds(128 * j, 128)]),
            ):
                block = effective(block, at, HALF + 128 * col)
                store(high, low, at, HALF + 128 * col, block)
                if col == j:
                    store(high, low, HALF + 128 * j, at, block.T)

    def hand_on(came, refs):
        passed = []
        for made, ref in zip(came, refs):
            made.wait_recv()
            passed.append(copy(ref, ref, mate))
        return passed

    local[0].wait()
    local[1].wait()
    for made in mate_x:
        made.wait_recv()
    own_rows(rows_x, xh, xl)
    passed_x = hand_on(cross_x, pieces(diag_x))
    local[2].wait()
    local[3].wait()
    for made in mate_k:
        made.wait_recv()
    own_rows(rows_k, kh, kl)
    for made in passed_x:
        made.wait_recv()
    far_rows(diag_x, xh, xl)
    passed_k = hand_on(cross_k, pieces(diag_k))
    for made in passed_k:
        made.wait_recv()
    far_rows(diag_k, kh, kl)
    local[4].wait()
    mate_g.wait_recv()
    passed_g = hand_on([cross_g], [rows_g.at[far]])
    passed_g[0].wait_recv()
    row = place_ids(h, 0, 0, 0, rows_g.shape)
    g_out[...] = jnp.where(row < size, rows_g[...].astype(F32), 0.0).astype(BF)
    for made in cross_x + cross_k + [cross_g] + mate_x + mate_k + [mate_g] + passed_x + passed_k + passed_g:
        made.wait_send()


def reduce_kernel(
    z_count,
    sizes, index, xh, xl, kh, kl, g, base, pair_hbm, start_hbm,
    diag_out, off_out, cross_out, schur_out, back_out,
    g_perm, panel, came_a, piece, came_z, schur, pair, near, nxt, nxt_came, start_f, yg, wide,
    s_high, s_low, t_high, t_low,
    local_sem, send_a, recv_a, send_z, recv_z, send_g, recv_g, send_p, recv_p, send_f, recv_f, send_l, recv_l,
):
    tm, ti, h, c = position()
    z = tm // PLANE
    p = tm - z * PLANE
    size = sizes[0]
    blocks = z_count * PLANE
    mate = (tm, ti + 1 - 2 * c)
    cross = (tm, lax.rem(ti + 2, 4))
    before = (lax.rem(tm + blocks - 1, blocks), ti)
    after = (lax.rem(tm + 1, blocks), ti)

    def plane_peer(k, sign):
        q = lax.rem(p + PLANE + sign * (k % PLANE), PLANE)
        return z * PLANE + q, q, lax.rem(h + k // PLANE, 2)

    def plane_device(k):
        t, q, hh = plane_peer(k, 1)
        return (t, 2 * hh + c)

    def z_device(k):
        return (lax.rem(z + k, z_count) * PLANE + p, ti)

    greet([mate, before, after])
    greet([plane_device(k) for k in range(1, 2 * PLANE)])
    greet([z_device(k) for k in range(1, z_count)])

    lane = lax.broadcasted_iota(jnp.int32, (128, 128), 0)
    for group in range(4):
        picks = index[:, pl.ds(128 * group, 128)] - 128 * group
        hot = jnp.where(lane == picks, 1.0, 0.0).astype(BF)
        columns = pl.ds(128 * group, 128)
        g_perm[:, columns] = dot(g[:, columns], hot).astype(BF)

    def first_step(u):
        return 2.0 * u - product(product(u, kh[...], kl[...]), xh[...], xl[...])

    def rest(v):
        w = product(v, kh[...], kl[...])
        return 2.0 * v - first_step(product(w, xh[...], xl[...]))

    own_cols = pl.ds(al(128 * ti, 128), 128)
    g_cols = g_perm[:, own_cols].astype(F32).T.astype(BF)
    v = first_step(dot(g_cols, xh[...]) + dot(g_cols, xl[...]))
    y_high, y_low = split(rest(v))
    panel[...] = dot(y_high, g_perm[...]) + dot(y_low, g_perm[...])

    pl.semaphore_wait(pltpu.get_barrier_semaphore(), 3 + 2 * PLANE - 1 + z_count - 1)

    def part(q):
        return pl.ds(al(16 * q, 16), 16)

    sends_a = []
    for k in range(1, PLANE):
        t, q, _ = plane_peer(k, 1)
        made = remote(panel.at[part(q)], came_a.at[p], send_a.at[k], recv_a.at[k], (t, ti))
        made.start()
        sends_a.append(made)
    came_a[p] = panel[part(p), :]

    mine = pl.ds(al(ROWS * c, 64), ROWS)
    v = first_step(xh[mine, :].astype(F32) + xl[mine, :].astype(F32))
    wide[...] = rest(v)

    for made in sends_a:
        made.wait_recv()
    total = came_a[0]
    for q in range(1, PLANE):
        total = total + came_a[q]
    piece[...] = total

    def tile_of(first, j):
        return pl.ds(al(first + 8 * (j // 4), 8), 8), pl.ds(al(128 * (j % 4), 128), 128)

    order = sorted(range(1, z_count), key=lambda k: -min(k, z_count - k))
    sends_z = []
    for k in order:
        device = z_device(k)
        j = lax.rem(z + k, z_count) // 2
        made = remote(piece.at[tile_of(0, j)], came_z.at[z], send_z.at[k], recv_z.at[k], device)
        made.start()
        sends_z.append(made)
    jz = z // 2
    tile_rows, tile_cols = tile_of(0, jz)
    came_z[z] = piece[tile_rows, tile_cols]

    far = pl.ds(al(HALF + ROWS * c, 64), ROWS)
    my_start = pl.ds(al(128 * ti, 128), 128)
    cross_start = pl.ds(al(128 * lax.rem(ti + 2, 4), 128), 128)
    cross_pair = remote(pair_hbm, pair.at[far], send_l.at[0], recv_l.at[0], cross)
    cross_pair.start()
    cross_s = remote(start_hbm, start_f.at[my_start], send_l.at[1], recv_l.at[1], cross)
    cross_s.start()
    mate_pair = remote(pair_hbm, pair.at[mine], send_l.at[2], recv_l.at[2], mate)
    mate_pair.start()
    mate_s = remote(start_hbm, start_f.at[my_start], send_l.at[3], recv_l.at[3], mate)
    mate_s.start()
    local_pair = pltpu.make_async_copy(pair_hbm, pair.at[mine], local_sem.at[0])
    local_pair.start()
    local_s = pltpu.make_async_copy(start_hbm, start_f.at[my_start], local_sem.at[1])
    local_s.start()

    wide_high, wide_low = split(wide[...])
    yg[...] = dot(wide_high, g_perm[...]) + dot(wide_low, g_perm[...])

    for made in sends_z:
        made.wait_recv()
    total = came_z[0]
    for q in range(1, z_count):
        total = total + came_z[q]
    tile_rows, tile_cols = tile_of(16 * p, jz)
    own_piece = 16 * (PLANE * ti + p)
    at_rows, at_cols = tile_of(own_piece, jz)
    schur[at_rows, at_cols] = total + base[tile_rows, tile_cols]
    sends_g = []
    for k in sorted(range(2, z_count, 2), key=lambda k: -min(k, z_count - k)):
        here = schur.at[at_rows, at_cols]
        made = remote(here, here, send_g.at[k], recv_g.at[k], z_device(k))
        made.start()
        sends_g.append(made)

    cross_pair.wait_recv()
    pass_pair = remote(pair.at[far], pair.at[far], send_l.at[4], recv_l.at[4], mate)
    pass_pair.start()
    local_pair.wait()
    mate_pair.wait_recv()
    pass_pair.wait_recv()
    row = place_ids(h, 0, 0, 0, pair.shape)
    near[...] = jnp.where(row < size, pair[...].astype(F32), 0.0).astype(BF)
    which = lax.broadcasted_iota(jnp.int32, (128, 512), 0)
    wanted = jnp.where(which < 64, which + 64 * ti, which + (256 - 64) + 64 * ti)
    hot = jnp.where(lax.broadcasted_iota(jnp.int32, (128, 512), 1) == wanted, 1.0, 0.0).astype(BF)
    u = dot_nt(hot, near[...]).astype(BF)
    v = first_step(dot(u, xh[...]) + dot(u, xl[...]))
    y_high, y_low = split(rest(v))
    to_near = dot(y_high, near[...]) + dot(y_low, near[...])
    to_glob = dot(y_high, g_perm[...]) + dot(y_low, g_perm[...])
    nxt[:, pl.ds(0, 256)] = to_near[0:64, 0:256]
    nxt[:, pl.ds(256, 512)] = to_glob[0:64, :]
    next_copy = remote(nxt, nxt_came, send_l.at[5], recv_l.at[5], before)
    next_copy.start()
    off_out[...] = to_near[0:64, 256:512]
    diag_out[...] = to_near[64:128, 256:512]
    cross_out[...] = to_glob[64:128, :]
    cross_s.wait_recv()
    pass_s = remote(start_f.at[cross_start], start_f.at[cross_start], send_l.at[6], recv_l.at[6], mate)
    pass_s.start()

    for made in sends_g:
        made.wait_recv()

    def piece_of(hh, cc, q):
        return schur.at[pl.ds(al(16 * (PLANE * (2 * hh + cc) + q), 16), 16)]

    here = piece_of(h, c, p)
    sends_p = []
    for k in (9, 10, 11, 12, 13, 14, 15, 2, 3, 4, 5, 6, 1, 7, 8):
        made = remote(here, here, send_p.at[k], recv_p.at[k], plane_device(k))
        made.start()
        sends_p.append((k, made))
    passed = remote(here, here, send_f.at[0], recv_f.at[0], mate)
    passed.start()
    sends_f = [passed]

    local_s.wait()
    mate_s.wait_recv()
    pass_s.wait_recv()
    s_high[...], s_low[...] = split(start_f[...])
    back = product(yg[...], s_high[...], s_low[...])
    yg[...] = back
    next_copy.wait_recv()
    last = jnp.where(tm == blocks - 1, 0.0, 1.0).astype(F32)
    diag_out[...] += nxt_came[:, pl.ds(0, 256)] * last
    cross_out[...] += nxt_came[:, pl.ds(256, 512)] * last

    for k, made in sends_p:
        made.wait_recv()
        _, q, hh = plane_peer(k, -1)
        came = piece_of(hh, c, q)
        passed = remote(came, came, send_f.at[k], recv_f.at[k], mate)
        passed.start()
        sends_f.append(passed)
    for made in sends_f:
        made.wait_recv()

    t_high[...], t_low[...] = split(schur[...])
    schur_out[...] = schur[my_start, :]
    inner = product(yg[...], t_high[...], t_low[...])
    back_out[...] = 2.0 * yg[...] - product(inner, s_high[...], s_low[...])

    for made in sends_a + sends_z + sends_g + sends_f + [made for _, made in sends_p]:
        made.wait_send()
    for made in (cross_pair, cross_s, mate_pair, mate_s, pass_pair, next_copy, pass_s):
        made.wait_send()


VM = pl.BlockSpec(memory_space=pltpu.VMEM)
ANY = pl.BlockSpec(memory_space=pl.ANY)
SM = pl.BlockSpec(memory_space=pltpu.SMEM)
DMA = pltpu.SemaphoreType.DMA


def shards(operator, initial, block_sizes, link_index, link_pair, link_global, schur_base, schur_start):
    order = operator.shape[2]
    z_count = lax.axis_size("tm") // PLANE
    whole = jax.ShapeDtypeStruct((order, order), BF)
    xh, xl, kh, kl, g = pl.pallas_call(
        gather_kernel,
        out_shape=[whole] * 4 + [jax.ShapeDtypeStruct((order, 512), BF)],
        in_specs=[SM, ANY, ANY, ANY],
        out_specs=[VM] * 5,
        scratch_shapes=[
            pltpu.VMEM((HALF, order), F32),
            pltpu.VMEM((HALF, order), F32),
            pltpu.VMEM((HALF, HALF), F32),
            pltpu.VMEM((HALF, HALF), F32),
            pltpu.VMEM((order, 512), BF),
            DMA((5,)),
            DMA((19,)),
            DMA((19,)),
        ],
        compiler_params=pltpu.CompilerParams(collective_id=0, has_side_effects=True),
        name="gather_blocks",
    )(block_sizes, operator[0], initial[0], link_global[0])
    out = pl.pallas_call(
        functools.partial(reduce_kernel, z_count),
        out_shape=[
            jax.ShapeDtypeStruct((64, 256), F32),
            jax.ShapeDtypeStruct((64, 256), F32),
            jax.ShapeDtypeStruct((64, 512), F32),
            jax.ShapeDtypeStruct((128, 512), F32),
            jax.ShapeDtypeStruct((ROWS, 512), F32),
        ],
        in_specs=[SM] + [VM] * 7 + [ANY, ANY],
        out_specs=[VM] * 5,
        scratch_shapes=[
            pltpu.VMEM((order, 512), BF),
            pltpu.VMEM((128, 512), F32),
            pltpu.VMEM((PLANE, 16, 512), F32),
            pltpu.VMEM((16, 512), F32),
            pltpu.VMEM((z_count, 8, 128), F32),
            pltpu.VMEM((512, 512), F32),
            pltpu.VMEM((order, 512), BF),
            pltpu.VMEM((order, 512), BF),
            pltpu.VMEM((64, order), F32),
            pltpu.VMEM((64, order), F32),
            pltpu.VMEM((512, 512), F32),
            pltpu.VMEM((ROWS, 512), F32),
            pltpu.VMEM((ROWS, order), F32),
            pltpu.VMEM((512, 512), BF),
            pltpu.VMEM((512, 512), BF),
            pltpu.VMEM((512, 512), BF),
            pltpu.VMEM((512, 512), BF),
            DMA((2,)),
            DMA((PLANE,)), DMA((PLANE,)),
            DMA((z_count,)), DMA((z_count,)),
            DMA((z_count,)), DMA((z_count,)),
            DMA((2 * PLANE,)), DMA((2 * PLANE,)),
            DMA((2 * PLANE,)), DMA((2 * PLANE,)),
            DMA((7,)), DMA((7,)),
        ],
        compiler_params=pltpu.CompilerParams(collective_id=1, has_side_effects=True),
        name="chain_and_reduce",
    )(block_sizes, link_index, xh, xl, kh, kl, g, schur_base, link_pair[0], schur_start)
    diag, off, cross, schur, back = out
    return diag[None], off[None], cross[None], schur, back[None]


def solution(mesh):
    return jax.shard_map(
        shards,
        mesh=mesh,
        in_specs=(
            P("tm", "tile", None),
            P("tm", "tile", None),
            P("tm"),
            P("tm", None),
            P("tm", "tile", None),
            P("tm", "tile", None),
            P("tile", None),
            P("tile", None),
        ),
        out_specs=(
            P("tm", "tile", None),
            P("tm", "tile", None),
            P("tm", "tile", None),
            P("tile", None),
            P("tm", "tile", None),
        ),
        check_vma=False,
    )
```

time: 808 us -> 88 us (0.11)
  waiting for transfers between devices: 741 us -> 0 us
  Pallas kernels: 0 us -> 79.4 us
  matrix products: 29.2 us -> 0 us
  between operations: 15.4 us -> 1.31 us
    psum x1 -> x0, waiting for transfers between devices: 474 us -> none  [shards(): totals = lax.psum(global_terms, ('tm', 'tile'))]
    all_gather x7 -> x0, waiting for transfers between devices: 184 us -> none  [the longest x2 58.8 us: shards(): lax.all_gather(x_rows, 'tile', axis=1, tiled=True)]
    pallas_call x0 -> x2, Pallas kernels: none -> 79.4 us  [the longest x1 55.8 us: shards(): pl.pallas_call(functools.partial(reduce_kernel, z_count), out_shape=[jax....]
    unnamed x10 -> x0, waiting for transfers between devices: 60.1 us -> none
    dot_general x14 -> x0, matrix products: 29.2 us -> none  [the longest x5 16.5 us: batched(): return jnp.einsum('bij,bjk->bik', left_side, right_side, precision=HIGH)]
    ppermute x1 -> x0, waiting for transfers between devices: 22.9 us -> none  [shifted_2(): return lax.ppermute(value, axis, pairs)]
  transfers between devices with their start and end apart: 10 -> 0, of which waited for: 10 -> 0; matrix products, arithmetic and copies ran while one was open for 4% -> 0% of each run, Pallas kernels for 0% -> 0%
where the time goes in v1:
time: 88 us; the launch traced here: 87.7 us
  Pallas kernels  79.4 us (90%)
  local copies, waits for them, and re-layouts  6.98 us (8%)
  between operations  1.31 us (1%)
    pallas_call x1, Pallas kernels, shards(): pl.pallas_call(functools.partial(reduce_kernel, z_count), out_shape=[jax....  55.8 us
    pallas_call x1, Pallas kernels, shards(): pl.pallas_call(gather_kernel, out_shape=[whole] * 4 + [jax.ShapeDtypeStru...  23.6 us
    unnamed x7, local copies, waits for them, and re-layouts  6.98 us

profile of v1, /device:TPU:1, one launch (start us, length us, event | category | flops | bytes accessed | tf_op | source)
XLA Modules:
  0.0 87.7 jit_solution(9648045707160446888)
XLA Ops:
  1.3 23.6 %gather_blocks.1 = (bf16[768,768]{1,0:T(8,128)(2,1)}, bf16[768,768]{1,0:T(8,128)(2,1)}, bf16[768,768]{1,0:T(8,128)(2,1)}, bf16[768,768]{1,0:T(8,128)(2,1)}, bf16[768,512]{1,0:T(8,128)(2,1)}) custom-call(s32[1]{0:T(128)S(6)} %copy.18.sizes, f32[192,768]{1,0:T(8,128)} %bitcast.8, f32[192,768]{1,0:T(8,128)} %bitcast.9, bf16[192,512]{1,0:T(8,128)(2,1)} %bitcast.12), custom_call_target="tpu_custom_call" | custom-call | tf_op jit(solution)/shard_map/gather_blocks/pallas_call | solution.py:408
  24.9 55.8 %chain_and_reduce.1 = (f32[64,256]{1,0:T(8,128)}, f32[64,256]{1,0:T(8,128)}, f32[64,512]{1,0:T(8,128)}, f32[128,512]{1,0:T(8,128)}, f32[192,512]{1,0:T(8,128)}) custom-call(s32[1]{0:T(128)S(6)} %copy.18.sizes, s32[1,512]{1,0:T(1,128)} %index.1, bf16[768,768]{1,0:T(8,128)(2,1)} %get-tuple-element.15.xh, bf16[768,768]{1,0:T(8,128)(2,1)} %get-tuple-element.16.xl, ...), custom_call_target="tpu_custom_call" | custom-call | tf_op jit(solution)/shard_map/chain_and_reduce/pallas_call | solution.py:426
  80.7 0.0 copy-start
  80.7 1.5 %copy.19 = f32[1,64,256]{2,1,0:T(8,128)} copy(f32[1,64,256]{2,1,0:T(8,128)} %bitcast.15) | data formatting | bytes 131072
  82.2 1.5 %copy.20 = f32[1,64,256]{2,1,0:T(8,128)} copy(f32[1,64,256]{2,1,0:T(8,128)} %bitcast.14) | data formatting | bytes 131072
  83.7 1.6 %copy.21 = f32[1,64,512]{2,1,0:T(8,128)} copy(f32[1,64,512]{2,1,0:T(8,128)} %bitcast.13) | data formatting | bytes 262144
  85.3 1.7 %copy.22 = f32[128,512]{1,0:T(8,128)} copy(f32[128,512]{1,0:T(8,128)} %get-tuple-element.33) | data formatting | bytes 524288
  86.9 0.0 copy-done
  86.9 0.7 copy.23
Async XLA Ops:
  80.7 6.2 %copy-start = (f32[192,512]{1,0:T(8,128)S(1)}, f32[192,512]{1,0:T(8,128)}, u32[]{:S(2)}) copy-start(f32[192,512]{1,0:T(8,128)} %get-tuple-element.24) | copy-start | bytes 1179652

commit v2 on v1

v2 whole, which is shorter than its diff:
```python
import functools

import jax
import jax.numpy as jnp
from jax import lax
from jax.experimental import pallas as pl
from jax.experimental.pallas import tpu as pltpu
from jax.sharding import PartitionSpec as P

MESH = pl.DeviceIdType.MESH
BF = jnp.bfloat16
F32 = jnp.float32
PLANE = 8
HALF = 384
ROWS = 192
GRANT = 32 << 20


def al(value, step):
    return pl.multiple_of(value, step)


def dot(left, right):
    return jnp.dot(left, right, preferred_element_type=F32)


def dot_nt(left, right):
    return lax.dot_general(left, right, (((1,), (1,)), ((), ())), preferred_element_type=F32)


def split(value):
    high = value.astype(BF)
    return high, (value - high.astype(F32)).astype(BF)


def product(value, high, low):
    value_high, value_low = split(value)
    return dot(value_high, high) + dot(value_high, low) + dot(value_low, high)


def position():
    tm = lax.axis_index("tm")
    ti = lax.axis_index("tile")
    h = ti // 2
    return tm, ti, h, ti - 2 * h


def remote(src, dst, send, recv, device):
    return pltpu.make_async_remote_copy(
        src_ref=src, dst_ref=dst, send_sem=send, recv_sem=recv, device_id=device, device_id_type=MESH
    )


def greet(devices):
    barrier = pltpu.get_barrier_semaphore()
    for device in devices:
        pl.semaphore_signal(barrier, inc=1, device_id=device, device_id_type=MESH)


def place_ids(h, first, axis, shape):
    ids = lax.broadcasted_iota(jnp.int32, shape, axis) + first
    return jnp.where(ids < HALF, ids + h * HALF, ids - h * HALF)


def block_kernel(
    z_count,
    sizes, k_hbm, x_hbm, g_hbm, pair_hbm, index_hbm, base_hbm, start_hbm,
    diag_out, off_out, cross_out, schur, w_out, s_high, s_low,
    xh, xl, kh, kl, rows_x, rows_k, diag_x, diag_k, rows_g, g_perm, index, base,
    panel, came_a, piece, came_z, pair, near, nxt, nxt_came, start_f, wide,
    local_sem, send_t, recv_t, send_a, recv_a, send_z, recv_z, send_g, recv_g, send_p, recv_p, send_f, recv_f, known,
):
    tm, ti, h, c = position()
    z = tm // PLANE
    p = tm - z * PLANE
    size = sizes[0]
    blocks = z_count * PLANE
    mate = (tm, ti + 1 - 2 * c)
    cross = (tm, lax.rem(ti + 2, 4))
    before = (lax.rem(tm + blocks - 1, blocks), ti)

    def plane_peer(k, sign):
        q = lax.rem(p + PLANE + sign * (k % PLANE), PLANE)
        return z * PLANE + q, q, lax.rem(h + k // PLANE, 2)

    def plane_device(k):
        t, q, hh = plane_peer(k, 1)
        return (t, 2 * hh + c)

    def z_device(k):
        return (lax.rem(z + k, z_count) * PLANE + p, ti)

    x_near = [plane_device(2), plane_device(PLANE - 2)]

    def z_near(by):
        return [z_device(by), z_device(z_count - by)]

    flip = p + 1 - 2 * lax.rem(p, 2)
    y_near = [(z * PLANE + flip, ti), (z * PLANE + flip, lax.rem(ti + 2, 4)), cross]
    greet(y_near + x_near + z_near(1) + [mate])

    def tell(round_, devices):
        for device in devices:
            pl.semaphore_signal(known.at[round_], inc=1, device_id=device, device_id_type=MESH)

    def hear(round_, count):
        pl.semaphore_wait(known.at[round_], count)

    own = al(h * HALF, 128)
    oth = al(HALF - h * HALF, 128)
    mine = pl.ds(al(ROWS * c, 64), ROWS)
    far = pl.ds(al(HALF + ROWS * c, 64), ROWS)
    my_start = pl.ds(al(128 * ti, 128), 128)
    cross_start = pl.ds(al(128 * lax.rem(ti + 2, 4), 128), 128)
    near_cols = pl.ds(al(256 * h, 256), 256)
    far_cols = pl.ds(al(256 - 256 * h, 256), 256)
    used = [0, 0]

    def copy(src, dst, device):
        at = used[0]
        used[0] += 1
        made = remote(src, dst, send_t.at[at], recv_t.at[at], device)
        made.start()
        sent.append(made)
        return made

    def local(src, dst):
        made = pltpu.make_async_copy(src, dst, local_sem.at[used[1]])
        used[1] += 1
        made.start()
        return made

    sent = []

    def pieces(ref):
        return [
            ref.at[pl.ds(al(256 * c, 128), 128), pl.ds(al(256 * c, 128), 128)],
            ref.at[pl.ds(al(256 * c, 128), 128), pl.ds(al(128 - 128 * c, 128), 128)],
            ref.at[pl.ds(al(128 + 64 * c, 64), 64), pl.ds(128, 256)],
        ]

    def sources(hbm):
        return [
            hbm.at[pl.ds(al(64 * c, 64), 128), pl.ds(al(own + 256 * c, 128), 128)],
            hbm.at[pl.ds(al(64 * c, 64), 128), pl.ds(al(own + 128 - 128 * c, 128), 128)],
            hbm.at[pl.ds(al(128 - 128 * c, 64), 64), pl.ds(al(own + 128, 128), 256)],
        ]

    def halves(hbm, rows):
        return [
            (hbm.at[:, pl.ds(own, HALF)], rows.at[mine, pl.ds(0, HALF)]),
            (hbm.at[:, pl.ds(oth, HALF)], rows.at[mine, pl.ds(HALF, HALF)]),
        ]

    local_g = local(g_hbm, rows_g.at[mine])
    local_x = [local(a, b) for a, b in halves(x_hbm, rows_x)]
    local_k = [local(a, b) for a, b in halves(k_hbm, rows_k)]
    local_index = local(index_hbm, index)
    local_pair = local(pair_hbm, pair.at[mine])
    local_base = local(base_hbm, base)
    local_s = local(start_hbm, start_f.at[my_start])

    pl.semaphore_wait(pltpu.get_barrier_semaphore(), 8)

    cross_g = copy(g_hbm.at[:, far_cols], rows_g.at[far, far_cols], cross)
    mate_g = copy(g_hbm, rows_g.at[mine], mate)
    cross_x = [copy(a, b, cross) for a, b in zip(sources(x_hbm), pieces(diag_x))]
    mate_x = [copy(a, b, mate) for a, b in halves(x_hbm, rows_x)]
    cross_k = [copy(a, b, cross) for a, b in zip(sources(k_hbm), pieces(diag_k))]
    mate_k = [copy(a, b, mate) for a, b in halves(k_hbm, rows_k)]
    cross_g_rest = copy(g_hbm.at[:, near_cols], rows_g.at[far, near_cols], cross)
    cross_pair = copy(pair_hbm, pair.at[far], cross)
    mate_pair = copy(pair_hbm, pair.at[mine], mate)
    tell(0, x_near)
    tell(1, z_near(1))

    def effective(block, first_row, first_col):
        row = place_ids(h, first_row, 0, block.shape)
        col = place_ids(h, first_col, 1, block.shape)
        unit = jnp.where(row == col, 1.0, 0.0).astype(F32)
        return jnp.where((row < size) & (col < size), block, unit)

    def store(high, low, row, col, value):
        n, m = value.shape
        value_high, value_low = split(value)
        high[pl.ds(row, n), pl.ds(col, m)] = value_high
        low[pl.ds(row, n), pl.ds(col, m)] = value_low

    def own_rows(rows, high, low):
        for i in range(3):
            at = 128 * i
            store(high, low, at, 0, effective(rows[pl.ds(at, 128), pl.ds(0, HALF)], at, 0))
            block = effective(rows[pl.ds(at, 128), pl.ds(HALF, HALF)], at, HALF)
            store(high, low, at, HALF, block)
            store(high, low, HALF, at, block.T)

    def far_rows(diag, high, low):
        for i in range(3):
            j = (i + 1) % 3
            at = HALF + 128 * i
            for col in (i, j):
                block = diag[pl.ds(128 * i, 128), pl.ds(128 * col, 128)]
                block = effective(block, at, HALF + 128 * col)
                store(high, low, at, HALF + 128 * col, block)
                if col == j:
                    store(high, low, HALF + 128 * j, at, block.T)

    def hand_on(came, refs):
        passed = []
        for made, ref in zip(came, refs):
            made.wait_recv()
            passed.append(copy(ref, ref, mate))
        return passed

    def arrive(copies):
        for made in copies:
            made.wait_recv()

    lane = lax.broadcasted_iota(jnp.int32, (128, 128), 0)

    def permute(first):
        columns = pl.ds(first, 128)
        hot = jnp.where(lane == index[:, columns] - first, 1.0, 0.0).astype(BF)
        picked = dot(rows_g[:, columns], hot)
        return jnp.where(place_ids(h, 0, 0, picked.shape) < size, picked, 0.0)

    def first_step(u):
        return 2.0 * u - product(product(u, kh[...], kl[...]), xh[...], xl[...])

    local_index.wait()
    local_g.wait()
    mate_g.wait_recv()
    pass_g = hand_on([cross_g], [rows_g.at[far, near_cols]])
    hear(0, 2)
    hear(1, 2)
    tell(2, x_near)
    tell(3, z_near(2))
    for made in local_x:
        made.wait()
    arrive(mate_x)
    own_rows(rows_x, xh, xl)
    arrive(pass_g)
    u = permute(al(128 * ti, 128)).T.astype(BF)
    pass_x = hand_on(cross_x, pieces(diag_x))
    hear(2, 2)
    hear(3, 2)
    tell(4, z_near(1))
    tell(5, z_near(4))
    for made in local_k:
        made.wait()
    arrive(mate_k)
    own_rows(rows_k, kh, kl)
    arrive(pass_x)
    far_rows(diag_x, xh, xl)
    v = dot(u, xh[...]) + dot(u, xl[...])
    pass_k = hand_on(cross_k, pieces(diag_k))
    arrive(pass_k)
    far_rows(diag_k, kh, kl)
    v = first_step(v)
    pass_g_rest = hand_on([cross_g_rest], [rows_g.at[far, far_cols]])
    w = product(product(v, kh[...], kl[...]), xh[...], xl[...])
    arrive(pass_g_rest)
    for group in range(4):
        g_perm[:, pl.ds(128 * group, 128)] = permute(128 * group).astype(BF)
    y_high, y_low = split(2.0 * v - first_step(w))
    pass_pair = hand_on([cross_pair], [pair.at[far]])
    panel[...] = dot(y_high, g_perm[...]) + dot(y_low, g_perm[...])

    hear(4, 2)
    hear(5, 2)

    def part(q):
        return pl.ds(al(16 * q, 16), 16)

    sends_a = []
    for k in range(1, PLANE):
        t, q, _ = plane_peer(k, 1)
        made = remote(panel.at[part(q)], came_a.at[p], send_a.at[k], recv_a.at[k], (t, ti))
        made.start()
        sends_a.append(made)
    came_a[p] = panel[part(p), :]

    local_pair.wait()
    mate_pair.wait_recv()
    arrive(pass_pair)
    row = place_ids(h, 0, 0, pair.shape)
    near[...] = jnp.where(row < size, pair[...].astype(F32), 0.0).astype(BF)
    which = lax.broadcasted_iota(jnp.int32, (128, 512), 0)
    wanted = jnp.where(which < 64, which + 64 * ti, which + (256 - 64) + 64 * ti)
    hot = jnp.where(lax.broadcasted_iota(jnp.int32, (128, 512), 1) == wanted, 1.0, 0.0).astype(BF)
    u = dot_nt(hot, near[...]).astype(BF)
    wide[pl.ds(0, 128), :] = first_step(dot(u, xh[...]) + dot(u, xl[...]))

    arrive(sends_a)
    total = came_a[0]
    for q in range(1, PLANE):
        total = total + came_a[q]
    piece[...] = total

    def tile_of(first, j):
        return pl.ds(al(first + 8 * (j // 4), 8), 8), pl.ds(al(128 * (j % 4), 128), 128)

    sends_z = []
    for k in sorted(range(1, z_count), key=lambda k: -min(k, z_count - k)):
        j = lax.rem(z + k, z_count) // 2
        made = remote(piece.at[tile_of(0, j)], came_z.at[z], send_z.at[k], recv_z.at[k], z_device(k))
        made.start()
        sends_z.append(made)
    jz = z // 2
    tile_rows, tile_cols = tile_of(0, jz)
    came_z[z] = piece[tile_rows, tile_cols]
    cross_s = copy(start_hbm, start_f.at[my_start], cross)
    mate_s = copy(start_hbm, start_f.at[my_start], mate)

    v = wide[pl.ds(0, 128), :]
    w = product(product(v, kh[...], kl[...]), xh[...], xl[...])
    y_high, y_low = split(2.0 * v - first_step(w))
    to_near = dot(y_high, near[...]) + dot(y_low, near[...])
    to_glob = dot(y_high, g_perm[...]) + dot(y_low, g_perm[...])
    nxt[:, pl.ds(0, 256)] = to_near[0:64, 0:256]
    nxt[:, pl.ds(256, 512)] = to_glob[0:64, :]
    next_copy = copy(nxt, nxt_came, before)
    off_out[...] = to_near[0:64, 256:512]
    diag_out[...] = to_near[64:128, 256:512]
    cross_out[...] = to_glob[64:128, :]
    local_base.wait()

    arrive(sends_z)
    total = came_z[0]
    for q in range(1, z_count):
        total = total + came_z[q]
    tile_rows, tile_cols = tile_of(16 * p, jz)
    at_rows, at_cols = tile_of(16 * (PLANE * ti + p), jz)
    schur[at_rows, at_cols] = total + base[tile_rows, tile_cols]
    sends_g = []
    for k in sorted(range(2, z_count, 2), key=lambda k: -min(k, z_count - k)):
        here = schur.at[at_rows, at_cols]
        made = remote(here, here, send_g.at[k], recv_g.at[k], z_device(k))
        made.start()
        sends_g.append(made)

    v = first_step(xh[mine, :].astype(F32) + xl[mine, :].astype(F32))
    pass_s = hand_on([cross_s], [start_f.at[cross_start]])
    w = product(product(v, kh[...], kl[...]), xh[...], xl[...])
    wide[...] = 2.0 * v - first_step(w)

    arrive(sends_g)

    def piece_of(hh, cc, q):
        return schur.at[pl.ds(al(16 * (PLANE * (2 * hh + cc) + q), 16), 16)]

    here = piece_of(h, c, p)
    sends_p = []
    for k in (9, 10, 11, 12, 13, 14, 15, 2, 3, 4, 5, 6, 1, 7, 8):
        made = remote(here, here, send_p.at[k], recv_p.at[k], plane_device(k))
        made.start()
        sends_p.append((k, made))
    passed = remote(here, here, send_f.at[0], recv_f.at[0], mate)
    passed.start()
    sends_f = [passed]

    wide_high, wide_low = split(wide[...])
    yg = dot(wide_high, g_perm[...]) + dot(wide_low, g_perm[...])
    local_s.wait()
    mate_s.wait_recv()
    arrive(pass_s)
    s_high[...], s_low[...] = split(start_f[...])
    w_out[...] = product(yg, s_high[...], s_low[...])

    for k, made in sends_p:
        made.wait_recv()
        _, q, hh = plane_peer(k, -1)
        came = piece_of(hh, c, q)
        passed = remote(came, came, send_f.at[k], recv_f.at[k], mate)
        passed.start()
        sends_f.append(passed)
    next_copy.wait_recv()
    last = jnp.where(tm == blocks - 1, 0.0, 1.0).astype(F32)
    diag_out[...] += nxt_came[:, pl.ds(0, 256)] * last
    cross_out[...] += nxt_came[:, pl.ds(256, 512)] * last
    arrive(sends_f)

    for made in sent + sends_a + sends_z + sends_g + sends_f + [made for _, made in sends_p]:
        made.wait_send()


def finish_kernel(
    diag, off, cross, schur, yg, s_high, s_low,
    diag_out, off_out, cross_out, schur_out, back_out,
    back, sem,
):
    mine = pl.ds(al(128 * lax.axis_index("tile"), 128), 128)
    pairs = ((diag, diag_out), (off, off_out), (cross, cross_out), (schur.at[mine], schur_out))
    copies = [pltpu.make_async_copy(a, b, sem.at[i]) for i, (a, b) in enumerate(pairs)]
    for made in copies:
        made.start()
    t_high, t_low = split(schur[...])
    for i in range(2):
        rows = pl.ds(96 * i, 96)
        inner = product(yg[rows, :], t_high, t_low)
        back[rows, :] = 2.0 * yg[rows, :] - product(inner, s_high[...], s_low[...])
        made = pltpu.make_async_copy(back.at[rows], back_out.at[rows], sem.at[4 + i])
        made.start()
        copies.append(made)
    for made in copies:
        made.wait()


VM = pl.BlockSpec(memory_space=pltpu.VMEM)
ANY = pl.BlockSpec(memory_space=pl.ANY)
HBM = pl.BlockSpec(memory_space=pltpu.HBM)
SM = pl.BlockSpec(memory_space=pltpu.SMEM)
DMA = pltpu.SemaphoreType.DMA


def shards(operator, initial, block_sizes, link_index, link_pair, link_global, schur_base, schur_start):
    order = operator.shape[2]
    z_count = lax.axis_size("tm") // PLANE
    out = pl.pallas_call(
        functools.partial(block_kernel, z_count),
        out_shape=[
            pltpu.VMEM((64, 256), F32),
            pltpu.VMEM((64, 256), F32),
            pltpu.VMEM((64, 512), F32),
            pltpu.VMEM((512, 512), F32),
            pltpu.VMEM((ROWS, 512), F32),
            pltpu.VMEM((512, 512), BF),
            pltpu.VMEM((512, 512), BF),
        ],
        in_specs=[SM] + [HBM] * 7,
        out_specs=[VM] * 7,
        scratch_shapes=[pltpu.VMEM((order, order), BF)] * 4
        + [pltpu.VMEM((HALF, order), F32)] * 2
        + [pltpu.VMEM((HALF, HALF), F32)] * 2
        + [
            pltpu.VMEM((order, 512), BF),
            pltpu.VMEM((order, 512), BF),
            pltpu.VMEM((1, 512), jnp.int32),
            pltpu.VMEM((128, 512), F32),
            pltpu.VMEM((128, 512), F32),
            pltpu.VMEM((PLANE, 16, 512), F32),
            pltpu.VMEM((16, 512), F32),
            pltpu.VMEM((z_count, 8, 128), F32),
            pltpu.VMEM((order, 512), BF),
            pltpu.VMEM((order, 512), BF),
            pltpu.VMEM((64, order), F32),
            pltpu.VMEM((64, order), F32),
            pltpu.VMEM((512, 512), F32),
            pltpu.VMEM((ROWS, order), F32),
            DMA((9,)),
            DMA((28,)), DMA((28,)),
            DMA((PLANE,)), DMA((PLANE,)),
            DMA((z_count,)), DMA((z_count,)),
            DMA((z_count,)), DMA((z_count,)),
            DMA((2 * PLANE,)), DMA((2 * PLANE,)),
            DMA((2 * PLANE,)), DMA((2 * PLANE,)),
            pltpu.SemaphoreType.REGULAR((6,)),
        ],
        compiler_params=pltpu.CompilerParams(collective_id=0, has_side_effects=True, vmem_limit_bytes=GRANT),
        name="block_step",
    )(
        block_sizes,
        *(
            pltpu.with_memory_space_constraint(array, pltpu.HBM)
            for array in (
                operator[0], initial[0], link_global[0], link_pair[0], link_index, schur_base, schur_start
            )
        ),
    )
    diag, off, cross, schur, back = pl.pallas_call(
        finish_kernel,
        out_shape=[
            jax.ShapeDtypeStruct((64, 256), F32),
            jax.ShapeDtypeStruct((64, 256), F32),
            jax.ShapeDtypeStruct((64, 512), F32),
            jax.ShapeDtypeStruct((128, 512), F32),
            jax.ShapeDtypeStruct((ROWS, 512), F32),
        ],
        in_specs=[VM] * 7,
        out_specs=[ANY] * 5,
        scratch_shapes=[pltpu.VMEM((ROWS, 512), F32), DMA((6,))],
        compiler_params=pltpu.CompilerParams(vmem_limit_bytes=GRANT),
        name="finish",
    )(*out)
    return diag[None], off[None], cross[None], schur, back[None]


def solution(mesh):
    return jax.shard_map(
        shards,
        mesh=mesh,
        in_specs=(
            P("tm", "tile", None),
            P("tm", "tile", None),
            P("tm"),
            P("tm", None),
            P("tm", "tile", None),
            P("tm", "tile", None),
            P("tile", None),
            P("tile", None),
        ),
        out_specs=(
            P("tm", "tile", None),
            P("tm", "tile", None),
            P("tm", "tile", None),
            P("tile", None),
            P("tm", "tile", None),
        ),
        check_vma=False,
    )
```

time: 88 us -> 70.7 us (0.80)
  Pallas kernels: 79.4 us -> 69.2 us
  local copies, waits for them, and re-layouts: 6.98 us -> 0 us
    pallas_call x2, Pallas kernels: 79.4 us -> 69.2 us  [the longest x1 67.1 us: shards(): pl.pallas_call(functools.partial(block_kernel, z_count), out_shape=[pltpu...]
    unnamed x7 -> x0, local copies, waits for them, and re-layouts: 6.98 us -> none
where the time goes in v2:
time: 70.7 us; the launch traced here: 70.6 us
  Pallas kernels  69.2 us (98%)
  between operations  1.45 us (2%)
    pallas_call x1, Pallas kernels, shards(): pl.pallas_call(functools.partial(block_kernel, z_count), out_shape=[pltpu...  67.1 us
    pallas_call x1, Pallas kernels, shards(): pl.pallas_call(finish_kernel, out_shape=[jax.ShapeDtypeStruct((64, 256),...  2.07 us

profile of v2, /device:TPU:1, one launch (start us, length us, event | category | flops | bytes accessed | tf_op | source)
XLA Modules:
  0.0 70.6 jit_solution(6125847941184707785)
XLA Ops:
  1.3 67.1 %block_step.1 = (f32[64,256]{1,0:T(8,128)S(1)}, f32[64,256]{1,0:T(8,128)S(1)}, f32[64,512]{1,0:T(8,128)S(1)}, f32[512,512]{1,0:T(8,128)S(1)}, f32[192,512]{1,0:T...) custom-call(s32[1]{0:T(128)S(6)} %copy.13.sizes, f32[192,768]{1,0:T(8,128)} %bitcast.8, ...), custom_call_target="tpu_custom_call" | custom-call | tf_op jit(solution)/shard_map/block_step/pallas_call | solution.py:419
  68.4 2.1 %finish.1 = (f32[64,256]{1,0:T(8,128)}, f32[64,256]{1,0:T(8,128)}, f32[64,512]{1,0:T(8,128)}, f32[128,512]{1,0:T(8,128)}, f32[192,512]{1,0:T(8,128)}) custom-call(f32[64,256]{1,0:T(8,128)S(1)} %get-tuple-element.17.diag, f32[64,256]{1,0:T(8,128)S(1)} %get-tuple-element.18.off, f32[64,512]{1,0:T(8,128)S(1)} %get-tuple-element.19.cross, ...), custom_call_target="tpu_custom_call" | custom-call | tf_op jit(solution)/shard_map/finish/pallas_call | solution.py:470

commit v3 on v2

--- a/solution.py
+++ b/solution.py
@@ -35,7 +35,11 @@
 
 def product(value, high, low):
     value_high, value_low = split(value)
-    return dot(value_high, high) + dot(value_high, low) + dot(value_low, high)
+    rows = value.shape[0]
+    if rows > 128:
+        return dot(value_high, high) + dot(value_high, low) + dot(value_low, high)
+    both = dot(jnp.concatenate([value_high, value_low], axis=0), high)
+    return both[:rows] + both[rows:] + dot(value_high, low)
 
 
 def position():
@@ -51,6 +55,10 @@
     )
 
 
+def drain(ref, sem):
+    pltpu.make_async_copy(ref, ref, sem).wait()
+
+
 def greet(devices):
     barrier = pltpu.get_barrier_semaphore()
     for device in devices:
@@ -65,15 +73,14 @@
 def block_kernel(
     z_count,
     sizes, k_hbm, x_hbm, g_hbm, pair_hbm, index_hbm, base_hbm, start_hbm,
-    diag_out, off_out, cross_out, schur, w_out, s_high, s_low,
+    diag_out, off_out, cross_out, schur, w_out, inner_out, s_high, s_low,
     xh, xl, kh, kl, rows_x, rows_k, diag_x, diag_k, rows_g, g_perm, index, base,
     panel, came_a, piece, came_z, pair, near, nxt, nxt_came, start_f, wide,
-    local_sem, send_t, recv_t, send_a, recv_a, send_z, recv_z, send_g, recv_g, send_p, recv_p, send_f, recv_f, known,
+    local_sem, send_sem, recv_t, recv_p, reduce_sem, known,
 ):
     tm, ti, h, c = position()
     z = tm // PLANE
     p = tm - z * PLANE
-    size = sizes[0]
     blocks = z_count * PLANE
     mate = (tm, ti + 1 - 2 * c)
     cross = (tm, lax.rem(ti + 2, 4))
@@ -116,21 +123,19 @@
     far_cols = pl.ds(al(256 - 256 * h, 256), 256)
     used = [0, 0]
 
-    def copy(src, dst, device):
-        at = used[0]
-        used[0] += 1
-        made = remote(src, dst, send_t.at[at], recv_t.at[at], device)
-        made.start()
-        sent.append(made)
-        return made
-
-    def local(src, dst):
-        made = pltpu.make_async_copy(src, dst, local_sem.at[used[1]])
-        used[1] += 1
+    def slot(kind):
+        used[kind] += 1
+        return used[kind] - 1
+
+    def copy(src, dst, device, group, at=None):
+        made = remote(src, dst, send_sem.at[group], recv_t.at[slot(0) if at is None else at], device)
         made.start()
         return made
 
-    sent = []
+    def local(src, dst, at=None):
+        made = pltpu.make_async_copy(src, dst, local_sem.at[slot(1) if at is None else at])
+        made.start()
+        return made
 
     def pieces(ref):
         return [
@@ -153,8 +158,11 @@
         ]
 
     local_g = local(g_hbm, rows_g.at[mine])
-    local_x = [local(a, b) for a, b in halves(x_hbm, rows_x)]
-    local_k = [local(a, b) for a, b in halves(k_hbm, rows_k)]
+    local_x, local_k = slot(1), slot(1)
+    for src, dst in halves(x_hbm, rows_x):
+        local(src, dst, local_x)
+    for src, dst in halves(k_hbm, rows_k):
+        local(src, dst, local_k)
     local_index = local(index_hbm, index)
     local_pair = local(pair_hbm, pair.at[mine])
     local_base = local(base_hbm, base)
@@ -162,15 +170,18 @@
 
     pl.semaphore_wait(pltpu.get_barrier_semaphore(), 8)
 
-    cross_g = copy(g_hbm.at[:, far_cols], rows_g.at[far, far_cols], cross)
-    mate_g = copy(g_hbm, rows_g.at[mine], mate)
-    cross_x = [copy(a, b, cross) for a, b in zip(sources(x_hbm), pieces(diag_x))]
-    mate_x = [copy(a, b, mate) for a, b in halves(x_hbm, rows_x)]
-    cross_k = [copy(a, b, cross) for a, b in zip(sources(k_hbm), pieces(diag_k))]
-    mate_k = [copy(a, b, mate) for a, b in halves(k_hbm, rows_k)]
-    cross_g_rest = copy(g_hbm.at[:, near_cols], rows_g.at[far, near_cols], cross)
-    cross_pair = copy(pair_hbm, pair.at[far], cross)
-    mate_pair = copy(pair_hbm, pair.at[mine], mate)
+    cross_g = copy(g_hbm.at[:, far_cols], rows_g.at[far, far_cols], cross, 0)
+    mate_g = copy(g_hbm, rows_g.at[mine], mate, 0)
+    cross_x = [copy(a, b, cross, 1) for a, b in zip(sources(x_hbm), pieces(diag_x))]
+    mate_x, mate_k, pass_x, pass_k = slot(0), slot(0), slot(0), slot(0)
+    for src, dst in halves(x_hbm, rows_x):
+        copy(src, dst, mate, 1, mate_x)
+    cross_k = [copy(a, b, cross, 2) for a, b in zip(sources(k_hbm), pieces(diag_k))]
+    for src, dst in halves(k_hbm, rows_k):
+        copy(src, dst, mate, 2, mate_k)
+    cross_g_rest = copy(g_hbm.at[:, near_cols], rows_g.at[far, near_cols], cross, 0)
+    cross_pair = copy(pair_hbm, pair.at[far], cross, 0)
+    mate_pair = copy(pair_hbm, pair.at[mine], mate, 0)
     tell(0, x_near)
     tell(1, z_near(1))
 
@@ -205,16 +216,9 @@
                 if col == j:
                     store(high, low, HALF + 128 * j, at, block.T)
 
-    def hand_on(came, refs):
-        passed = []
-        for made, ref in zip(came, refs):
-            made.wait_recv()
-            passed.append(copy(ref, ref, mate))
-        return passed
-
-    def arrive(copies):
-        for made in copies:
-            made.wait_recv()
+    def hand_on(came, ref, group=3, at=None):
+        came.wait_recv()
+        return copy(ref, ref, mate, group, at)
 
     lane = lax.broadcasted_iota(jnp.int32, (128, 128), 0)
 
@@ -227,43 +231,44 @@
     def first_step(u):
         return 2.0 * u - product(product(u, kh[...], kl[...]), xh[...], xl[...])
 
+    size = sizes[0]
     local_index.wait()
     local_g.wait()
     mate_g.wait_recv()
-    pass_g = hand_on([cross_g], [rows_g.at[far, near_cols]])
+    pass_g = hand_on(cross_g, rows_g.at[far, near_cols])
     hear(0, 2)
     hear(1, 2)
     tell(2, x_near)
     tell(3, z_near(2))
-    for made in local_x:
-        made.wait()
-    arrive(mate_x)
+    drain(rows_x.at[mine], local_sem.at[local_x])
+    drain(rows_x.at[mine], recv_t.at[mate_x])
     own_rows(rows_x, xh, xl)
-    arrive(pass_g)
+    pass_g.wait_recv()
     u = permute(al(128 * ti, 128)).T.astype(BF)
-    pass_x = hand_on(cross_x, pieces(diag_x))
+    for made, ref in zip(cross_x, pieces(diag_x)):
+        hand_on(made, ref, 3, pass_x)
     hear(2, 2)
     hear(3, 2)
     tell(4, z_near(1))
     tell(5, z_near(4))
-    for made in local_k:
-        made.wait()
-    arrive(mate_k)
+    drain(rows_k.at[mine], local_sem.at[local_k])
+    drain(rows_k.at[mine], recv_t.at[mate_k])
     own_rows(rows_k, kh, kl)
-    arrive(pass_x)
+    drain(rows_x.at[pl.ds(0, 64)], recv_t.at[pass_x])
     far_rows(diag_x, xh, xl)
     v = dot(u, xh[...]) + dot(u, xl[...])
-    pass_k = hand_on(cross_k, pieces(diag_k))
-    arrive(pass_k)
+    for made, ref in zip(cross_k, pieces(diag_k)):
+        hand_on(made, ref, 3, pass_k)
+    drain(rows_x.at[pl.ds(0, 64)], recv_t.at[pass_k])
     far_rows(diag_k, kh, kl)
     v = first_step(v)
-    pass_g_rest = hand_on([cross_g_rest], [rows_g.at[far, far_cols]])
+    pass_g_rest = hand_on(cross_g_rest, rows_g.at[far, far_cols])
     w = product(product(v, kh[...], kl[...]), xh[...], xl[...])
-    arrive(pass_g_rest)
+    pass_g_rest.wait_recv()
     for group in range(4):
         g_perm[:, pl.ds(128 * group, 128)] = permute(128 * group).astype(BF)
     y_high, y_low = split(2.0 * v - first_step(w))
-    pass_pair = hand_on([cross_pair], [pair.at[far]])
+    pass_pair = hand_on(cross_pair, pair.at[far])
     panel[...] = dot(y_high, g_perm[...]) + dot(y_low, g_perm[...])
 
     hear(4, 2)
@@ -272,17 +277,14 @@
     def part(q):
         return pl.ds(al(16 * q, 16), 16)
 
-    sends_a = []
     for k in range(1, PLANE):
         t, q, _ = plane_peer(k, 1)
-        made = remote(panel.at[part(q)], came_a.at[p], send_a.at[k], recv_a.at[k], (t, ti))
-        made.start()
-        sends_a.append(made)
+        remote(panel.at[part(q)], came_a.at[p], reduce_sem.at[0], reduce_sem.at[1], (t, ti)).start()
     came_a[p] = panel[part(p), :]
 
     local_pair.wait()
     mate_pair.wait_recv()
-    arrive(pass_pair)
+    pass_pair.wait_recv()
     row = place_ids(h, 0, 0, pair.shape)
     near[...] = jnp.where(row < size, pair[...].astype(F32), 0.0).astype(BF)
     which = lax.broadcasted_iota(jnp.int32, (128, 512), 0)
@@ -291,7 +293,8 @@
     u = dot_nt(hot, near[...]).astype(BF)
     wide[pl.ds(0, 128), :] = first_step(dot(u, xh[...]) + dot(u, xl[...]))
 
-    arrive(sends_a)
+    others_a = came_a.at[pl.ds(0, PLANE - 1)]
+    drain(others_a, reduce_sem.at[1])
     total = came_a[0]
     for q in range(1, PLANE):
         total = total + came_a[q]
@@ -300,17 +303,14 @@
     def tile_of(first, j):
         return pl.ds(al(first + 8 * (j // 4), 8), 8), pl.ds(al(128 * (j % 4), 128), 128)
 
-    sends_z = []
     for k in sorted(range(1, z_count), key=lambda k: -min(k, z_count - k)):
         j = lax.rem(z + k, z_count) // 2
-        made = remote(piece.at[tile_of(0, j)], came_z.at[z], send_z.at[k], recv_z.at[k], z_device(k))
-        made.start()
-        sends_z.append(made)
+        remote(piece.at[tile_of(0, j)], came_z.at[z], reduce_sem.at[2], reduce_sem.at[3], z_device(k)).start()
     jz = z // 2
     tile_rows, tile_cols = tile_of(0, jz)
     came_z[z] = piece[tile_rows, tile_cols]
-    cross_s = copy(start_hbm, start_f.at[my_start], cross)
-    mate_s = copy(start_hbm, start_f.at[my_start], mate)
+    cross_s = copy(start_hbm, start_f.at[my_start], cross, 4)
+    mate_s = copy(start_hbm, start_f.at[my_start], mate, 4)
 
     v = wide[pl.ds(0, 128), :]
     w = product(product(v, kh[...], kl[...]), xh[...], xl[...])
@@ -319,32 +319,31 @@
     to_glob = dot(y_high, g_perm[...]) + dot(y_low, g_perm[...])
     nxt[:, pl.ds(0, 256)] = to_near[0:64, 0:256]
     nxt[:, pl.ds(256, 512)] = to_glob[0:64, :]
-    next_copy = copy(nxt, nxt_came, before)
+    next_copy = copy(nxt, nxt_came, before, 5)
     off_out[...] = to_near[0:64, 256:512]
     diag_out[...] = to_near[64:128, 256:512]
     cross_out[...] = to_glob[64:128, :]
     local_base.wait()
-
-    arrive(sends_z)
+    wide[...] = first_step(xh[mine, :].astype(F32) + xl[mine, :].astype(F32))
+
+    others_z = came_z.at[pl.ds(0, z_count - 1)]
+    drain(others_z, reduce_sem.at[3])
     total = came_z[0]
     for q in range(1, z_count):
         total = total + came_z[q]
     tile_rows, tile_cols = tile_of(16 * p, jz)
     at_rows, at_cols = tile_of(16 * (PLANE * ti + p), jz)
     schur[at_rows, at_cols] = total + base[tile_rows, tile_cols]
-    sends_g = []
     for k in sorted(range(2, z_count, 2), key=lambda k: -min(k, z_count - k)):
         here = schur.at[at_rows, at_cols]
-        made = remote(here, here, send_g.at[k], recv_g.at[k], z_device(k))
-        made.start()
-        sends_g.append(made)
-
-    v = first_step(xh[mine, :].astype(F32) + xl[mine, :].astype(F32))
-    pass_s = hand_on([cross_s], [start_f.at[cross_start]])
+        remote(here, here, reduce_sem.at[4], reduce_sem.at[5], z_device(k)).start()
+
+    v = wide[...]
     w = product(product(v, kh[...], kl[...]), xh[...], xl[...])
     wide[...] = 2.0 * v - first_step(w)
 
-    arrive(sends_g)
+    others_g = came_z.at[pl.ds(0, z_count // 2 - 1)]
+    drain(others_g, reduce_sem.at[5])
 
     def piece_of(hh, cc, q):
         return schur.at[pl.ds(al(16 * (PLANE * (2 * hh + cc) + q), 16), 16)]
@@ -352,18 +351,17 @@
     here = piece_of(h, c, p)
     sends_p = []
     for k in (9, 10, 11, 12, 13, 14, 15, 2, 3, 4, 5, 6, 1, 7, 8):
-        made = remote(here, here, send_p.at[k], recv_p.at[k], plane_device(k))
+        made = remote(here, here, reduce_sem.at[6], recv_p.at[k], plane_device(k))
         made.start()
         sends_p.append((k, made))
-    passed = remote(here, here, send_f.at[0], recv_f.at[0], mate)
-    passed.start()
-    sends_f = [passed]
+    remote(here, here, reduce_sem.at[7], reduce_sem.at[8], mate).start()
+    pass_s = hand_on(cross_s, start_f.at[cross_start], 4)
 
     wide_high, wide_low = split(wide[...])
     yg = dot(wide_high, g_perm[...]) + dot(wide_low, g_perm[...])
     local_s.wait()
     mate_s.wait_recv()
-    arrive(pass_s)
+    pass_s.wait_recv()
     s_high[...], s_low[...] = split(start_f[...])
     w_out[...] = product(yg, s_high[...], s_low[...])
 
@@ -371,21 +369,35 @@
         made.wait_recv()
         _, q, hh = plane_peer(k, -1)
         came = piece_of(hh, c, q)
-        passed = remote(came, came, send_f.at[k], recv_f.at[k], mate)
-        passed.start()
-        sends_f.append(passed)
+        remote(came, came, reduce_sem.at[7], reduce_sem.at[8], mate).start()
+    inner_out[...] = half_inner(c, w_out, schur)
     next_copy.wait_recv()
     last = jnp.where(tm == blocks - 1, 0.0, 1.0).astype(F32)
     diag_out[...] += nxt_came[:, pl.ds(0, 256)] * last
     cross_out[...] += nxt_came[:, pl.ds(256, 512)] * last
-    arrive(sends_f)
-
-    for made in sent + sends_a + sends_z + sends_g + sends_f + [made for _, made in sends_p]:
-        made.wait_send()
+    others_p = schur.at[pl.ds(0, 16 * (2 * PLANE - 1))]
+    everything = schur.at[pl.ds(0, 32 * PLANE)]
+    drain(everything, reduce_sem.at[8])
+
+    for group in range(5):
+        drain(rows_x.at[pl.ds(0, 256)], send_sem.at[group])
+    next_copy.wait_send()
+    drain(others_a, reduce_sem.at[0])
+    drain(others_z, reduce_sem.at[2])
+    drain(others_g, reduce_sem.at[4])
+    drain(others_p, reduce_sem.at[6])
+    drain(everything, reduce_sem.at[7])
+
+
+def half_inner(which, w, schur):
+    first = pl.ds(al(128 * which, 128), 128)
+    second = pl.ds(al(256 + 128 * which, 128), 128)
+    t_high, t_low = split(jnp.concatenate([schur[first, :], schur[second, :]], axis=0))
+    return product(jnp.concatenate([w[:, first], w[:, second]], axis=1), t_high, t_low)
 
 
 def finish_kernel(
-    diag, off, cross, schur, yg, s_high, s_low,
+    diag, off, cross, schur, w, inner, s_high, s_low,
     diag_out, off_out, cross_out, schur_out, back_out,
     back, sem,
 ):
@@ -394,11 +406,11 @@
     copies = [pltpu.make_async_copy(a, b, sem.at[i]) for i, (a, b) in enumerate(pairs)]
     for made in copies:
         made.start()
-    t_high, t_low = split(schur[...])
+    ti = lax.axis_index("tile")
+    whole = inner[...] + half_inner(1 - lax.rem(ti, 2), w, schur)
     for i in range(2):
         rows = pl.ds(96 * i, 96)
-        inner = product(yg[rows, :], t_high, t_low)
-        back[rows, :] = 2.0 * yg[rows, :] - product(inner, s_high[...], s_low[...])
+        back[rows, :] = 2.0 * w[rows, :] - product(whole[96 * i : 96 * (i + 1)], s_high[...], s_low[...])
         made = pltpu.make_async_copy(back.at[rows], back_out.at[rows], sem.at[4 + i])
         made.start()
         copies.append(made)
@@ -407,9 +419,9 @@
 
 
 VM = pl.BlockSpec(memory_space=pltpu.VMEM)
+SM = pl.BlockSpec(memory_space=pltpu.SMEM)
 ANY = pl.BlockSpec(memory_space=pl.ANY)
 HBM = pl.BlockSpec(memory_space=pltpu.HBM)
-SM = pl.BlockSpec(memory_space=pltpu.SMEM)
 DMA = pltpu.SemaphoreType.DMA
 
 
@@ -424,11 +436,12 @@
             pltpu.VMEM((64, 512), F32),
             pltpu.VMEM((512, 512), F32),
             pltpu.VMEM((ROWS, 512), F32),
+            pltpu.VMEM((ROWS, 512), F32),
             pltpu.VMEM((512, 512), BF),
             pltpu.VMEM((512, 512), BF),
         ],
         in_specs=[SM] + [HBM] * 7,
-        out_specs=[VM] * 7,
+        out_specs=[VM] * 8,
         scratch_shapes=[pltpu.VMEM((order, order), BF)] * 4
         + [pltpu.VMEM((HALF, order), F32)] * 2
         + [pltpu.VMEM((HALF, HALF), F32)] * 2
@@ -447,13 +460,11 @@
             pltpu.VMEM((64, order), F32),
             pltpu.VMEM((512, 512), F32),
             pltpu.VMEM((ROWS, order), F32),
+            DMA((7,)),
+            DMA((6,)),
+            DMA((22,)),
+            DMA((2 * PLANE,)),
             DMA((9,)),
-            DMA((28,)), DMA((28,)),
-            DMA((PLANE,)), DMA((PLANE,)),
-            DMA((z_count,)), DMA((z_count,)),
-            DMA((z_count,)), DMA((z_count,)),
-            DMA((2 * PLANE,)), DMA((2 * PLANE,)),
-            DMA((2 * PLANE,)), DMA((2 * PLANE,)),
             pltpu.SemaphoreType.REGULAR((6,)),
         ],
         compiler_params=pltpu.CompilerParams(collective_id=0, has_side_effects=True, vmem_limit_bytes=GRANT),
@@ -476,7 +487,7 @@
             jax.ShapeDtypeStruct((128, 512), F32),
             jax.ShapeDtypeStruct((ROWS, 512), F32),
         ],
-        in_specs=[VM] * 7,
+        in_specs=[VM] * 8,
         out_specs=[ANY] * 5,
         scratch_shapes=[pltpu.VMEM((ROWS, 512), F32), DMA((6,))],
         compiler_params=pltpu.CompilerParams(vmem_limit_bytes=GRANT),

time: 70.7 us -> 65.5 us (0.926)
  Pallas kernels: 69.2 us -> 63.9 us
    pallas_call x1, Pallas kernels: 67.1 us -> 62.4 us  [shards(): pl.pallas_call(functools.partial(block_kernel, z_count), out_shape=[pltpu...]
where the time goes in v3:
time: 65.5 us; the launch traced here: 65.4 us
  Pallas kernels  63.9 us (98%)
  between operations  1.45 us (2%)
    pallas_call x1, Pallas kernels, shards(): pl.pallas_call(functools.partial(block_kernel, z_count), out_shape=[pltpu...  62.4 us
    pallas_call x1, Pallas kernels, shards(): pl.pallas_call(finish_kernel, out_shape=[jax.ShapeDtypeStruct((64, 256),...  1.54 us

profile of v3, /device:TPU:1, one launch (start us, length us, event | category | flops | bytes accessed | tf_op | source)
XLA Modules:
  0.0 65.4 jit_solution(14237107931212606132)
XLA Ops:
  1.3 62.4 %block_step.1 = (f32[64,256]{1,0:T(8,128)S(1)}, f32[64,256]{1,0:T(8,128)S(1)}, f32[64,512]{1,0:T(8,128)S(1)}, f32[512,512]{1,0:T(8,128)S(1)}, f32[192,512]{1,0:T...) custom-call(s32[1]{0:T(128)S(6)} %copy.13.sizes, ...), custom_call_target="tpu_custom_call" | custom-call | tf_op jit(solution)/shard_map/block_step/pallas_call | solution.py:431
  63.7 1.5 %finish.1 = (f32[64,256]{1,0:T(8,128)}, f32[64,256]{1,0:T(8,128)}, f32[64,512]{1,0:T(8,128)}, f32[128,512]{1,0:T(8,128)}, f32[192,512]{1,0:T(8,128)}) custom-call(f32[64,256]{1,0:T(8,128)S(1)} %get-tuple-element.18.diag, f32[64,256]{1,0:T(8,128)S(1)} %get-tuple-element.19.off, f32[64,512]{1,0:T(8,128)S(1)} %get-tuple-element.20.cross, ...), custom_call_target="tpu_custom_call" | custom-call | tf_op jit(solution)/shard_map/finish/pallas_call | solution.py:481

commit v4 on v3

--- a/solution.py
+++ b/solution.py
@@ -14,6 +14,8 @@
 HALF = 384
 ROWS = 192
 GRANT = 32 << 20
+COMES = (0, 1, 2, 7, 6, 3, 4, 5)
+EARLY = 5
 
 
 def al(value, step):
@@ -75,7 +77,7 @@
     sizes, k_hbm, x_hbm, g_hbm, pair_hbm, index_hbm, base_hbm, start_hbm,
     diag_out, off_out, cross_out, schur, w_out, inner_out, s_high, s_low,
     xh, xl, kh, kl, rows_x, rows_k, diag_x, diag_k, rows_g, g_perm, index, base,
-    panel, came_a, piece, came_z, pair, near, nxt, nxt_came, start_f, wide,
+    panel, came_a, piece, came_z, tiles, pair, near, nxt, nxt_came, start_f, wide,
     local_sem, send_sem, recv_t, recv_p, reduce_sem, known,
 ):
     tm, ti, h, c = position()
@@ -257,11 +259,15 @@
     drain(rows_x.at[pl.ds(0, 64)], recv_t.at[pass_x])
     far_rows(diag_x, xh, xl)
     v = dot(u, xh[...]) + dot(u, xl[...])
+    w_own = product(v, kh[:, pl.ds(0, HALF)], kl[:, pl.ds(0, HALF)])
+    first, second = pl.ds(0, HALF), pl.ds(HALF, HALF)
+    w_far = product(v[:, :HALF], kh[first, second], kl[first, second])
     for made, ref in zip(cross_k, pieces(diag_k)):
         hand_on(made, ref, 3, pass_k)
     drain(rows_x.at[pl.ds(0, 64)], recv_t.at[pass_k])
     far_rows(diag_k, kh, kl)
-    v = first_step(v)
+    w_far = w_far + product(v[:, HALF:], kh[second, second], kl[second, second])
+    v = 2.0 * v - product(jnp.concatenate([w_own, w_far], axis=1), xh[...], xl[...])
     pass_g_rest = hand_on(cross_g_rest, rows_g.at[far, far_cols])
     w = product(product(v, kh[...], kl[...]), xh[...], xl[...])
     pass_g_rest.wait_recv()
@@ -309,7 +315,7 @@
     jz = z // 2
     tile_rows, tile_cols = tile_of(0, jz)
     came_z[z] = piece[tile_rows, tile_cols]
-    cross_s = copy(start_hbm, start_f.at[my_start], cross, 4)
+    cross_s = copy(start_hbm.at[:, near_cols], start_f.at[my_start, near_cols], cross, 4)
     mate_s = copy(start_hbm, start_f.at[my_start], mate, 4)
 
     v = wide[pl.ds(0, 128), :]
@@ -332,44 +338,71 @@
     for q in range(1, z_count):
         total = total + came_z[q]
     tile_rows, tile_cols = tile_of(16 * p, jz)
-    at_rows, at_cols = tile_of(16 * (PLANE * ti + p), jz)
-    schur[at_rows, at_cols] = total + base[tile_rows, tile_cols]
+    own_piece = PLANE * ti + p
+    tiles[own_piece, 0] = total + base[tile_rows, tile_cols]
     for k in sorted(range(2, z_count, 2), key=lambda k: -min(k, z_count - k)):
-        here = schur.at[at_rows, at_cols]
-        remote(here, here, reduce_sem.at[4], reduce_sem.at[5], z_device(k)).start()
+        at = COMES.index((z_count - k) // 2)
+        late = 1 if at >= EARLY else 0
+        here = tiles.at[own_piece, 0]
+        remote(here, tiles.at[own_piece, at], reduce_sem.at[4], reduce_sem.at[9 + late], z_device(k)).start()
+
+    def piece_of(hh, cc, q, wave):
+        return tiles.at[PLANE * (2 * hh + cc) + q, pl.ds(0, EARLY) if wave == 0 else pl.ds(EARLY, 8 - EARLY)]
+
+    order = (9, 10, 11, 12, 13, 14, 15, 2, 3, 4, 5, 6, 1, 7, 8)
+
+    def spread(wave):
+        here = piece_of(h, c, p, wave)
+        came = []
+        for k in order:
+            made = remote(here, here, reduce_sem.at[6], recv_p.at[16 * wave + k], plane_device(k))
+            made.start()
+            came.append((k, made))
+        remote(here, here, reduce_sem.at[7], reduce_sem.at[8], mate).start()
+        return came
+
+    def hand_over(came, wave):
+        for k, made in came:
+            made.wait_recv()
+            _, q, hh = plane_peer(k, -1)
+            ref = piece_of(hh, c, q, wave)
+            remote(ref, ref, reduce_sem.at[7], reduce_sem.at[8], mate).start()
 
     v = wide[...]
     w = product(product(v, kh[...], kl[...]), xh[...], xl[...])
+    drain(came_z.at[pl.ds(0, EARLY - 1)], reduce_sem.at[9])
+    first_wave = spread(0)
     wide[...] = 2.0 * v - first_step(w)
-
-    others_g = came_z.at[pl.ds(0, z_count // 2 - 1)]
-    drain(others_g, reduce_sem.at[5])
-
-    def piece_of(hh, cc, q):
-        return schur.at[pl.ds(al(16 * (PLANE * (2 * hh + cc) + q), 16), 16)]
-
-    here = piece_of(h, c, p)
-    sends_p = []
-    for k in (9, 10, 11, 12, 13, 14, 15, 2, 3, 4, 5, 6, 1, 7, 8):
-        made = remote(here, here, reduce_sem.at[6], recv_p.at[k], plane_device(k))
-        made.start()
-        sends_p.append((k, made))
-    remote(here, here, reduce_sem.at[7], reduce_sem.at[8], mate).start()
-    pass_s = hand_on(cross_s, start_f.at[cross_start], 4)
+    pass_s = hand_on(cross_s, start_f.at[cross_start, far_cols], 4)
+    drain(came_z.at[pl.ds(0, 8 - EARLY)], reduce_sem.at[10])
+    second_wave = spread(1)
 
     wide_high, wide_low = split(wide[...])
     yg = dot(wide_high, g_perm[...]) + dot(wide_low, g_perm[...])
     local_s.wait()
     mate_s.wait_recv()
     pass_s.wait_recv()
+    start_f[far_cols, near_cols] = start_f[near_cols, far_cols].T
     s_high[...], s_low[...] = split(start_f[...])
     w_out[...] = product(yg, s_high[...], s_low[...])
 
-    for k, made in sends_p:
-        made.wait_recv()
-        _, q, hh = plane_peer(k, -1)
-        came = piece_of(hh, c, q)
-        remote(came, came, reduce_sem.at[7], reduce_sem.at[8], mate).start()
+    places = [lax.rem(jz + step, 8) for step in COMES]
+    places = [(8 * (j // 4), al(128 * (j % 4), 128)) for j in places]
+
+    def lay_out(cc, slots):
+        def body(i, carry):
+            q = PLANE * (2 * (i // PLANE) + cc) + lax.rem(i, PLANE)
+            for at in slots:
+                row, col = places[at]
+                schur[pl.ds(al(16 * q + row, 8), 8), pl.ds(col, 128)] = tiles[q, at]
+            return carry
+
+        lax.fori_loop(0, 2 * PLANE, body, 0)
+
+    hand_over(first_wave, 0)
+    lay_out(c, range(EARLY))
+    hand_over(second_wave, 1)
+    lay_out(c, range(EARLY, 8))
     inner_out[...] = half_inner(c, w_out, schur)
     next_copy.wait_recv()
     last = jnp.where(tm == blocks - 1, 0.0, 1.0).astype(F32)
@@ -378,13 +411,15 @@
     others_p = schur.at[pl.ds(0, 16 * (2 * PLANE - 1))]
     everything = schur.at[pl.ds(0, 32 * PLANE)]
     drain(everything, reduce_sem.at[8])
-
-    for group in range(5):
+    lay_out(1 - c, range(8))
+
+    for group in range(4):
         drain(rows_x.at[pl.ds(0, 256)], send_sem.at[group])
+    drain(start_f.at[pl.ds(0, 256)], send_sem.at[4])
     next_copy.wait_send()
     drain(others_a, reduce_sem.at[0])
     drain(others_z, reduce_sem.at[2])
-    drain(others_g, reduce_sem.at[4])
+    drain(came_z.at[pl.ds(0, z_count // 2 - 1)], reduce_sem.at[4])
     drain(others_p, reduce_sem.at[6])
     drain(everything, reduce_sem.at[7])
 
@@ -454,6 +489,7 @@
             pltpu.VMEM((PLANE, 16, 512), F32),
             pltpu.VMEM((16, 512), F32),
             pltpu.VMEM((z_count, 8, 128), F32),
+            pltpu.VMEM((4 * PLANE, 8, 8, 128), F32),
             pltpu.VMEM((order, 512), BF),
             pltpu.VMEM((order, 512), BF),
             pltpu.VMEM((64, order), F32),
@@ -463,8 +499,8 @@
             DMA((7,)),
             DMA((6,)),
             DMA((22,)),
-            DMA((2 * PLANE,)),
-            DMA((9,)),
+            DMA((4 * PLANE,)),
+            DMA((11,)),
             pltpu.SemaphoreType.REGULAR((6,)),
         ],
         compiler_params=pltpu.CompilerParams(collective_id=0, has_side_effects=True, vmem_limit_bytes=GRANT),

time: 65.5 us -> 64.5 us (0.985)
  Pallas kernels: 63.9 us -> 62.9 us
    pallas_call x1, Pallas kernels: 62.4 us -> 61.4 us  [shards(): pl.pallas_call(functools.partial(block_kernel, z_count), out_shape=[pltpu...]
where the time goes in v4:
time: 64.5 us; the launch traced here: 64.4 us
  Pallas kernels  62.9 us (98%)
  between operations  1.45 us (2%)
    pallas_call x1, Pallas kernels, shards(): pl.pallas_call(functools.partial(block_kernel, z_count), out_shape=[pltpu...  61.4 us
    pallas_call x1, Pallas kernels, shards(): pl.pallas_call(finish_kernel, out_shape=[jax.ShapeDtypeStruct((64, 256),...  1.54 us

profile of v4, /device:TPU:1, one launch (start us, length us, event | category | flops | bytes accessed | tf_op | source)
XLA Modules:
  0.0 64.4 jit_solution(2191463005006873277)
XLA Ops:
  1.3 61.4 %block_step.1 = (f32[64,256]{1,0:T(8,128)S(1)}, f32[64,256]{1,0:T(8,128)S(1)}, f32[64,512]{1,0:T(8,128)S(1)}, f32[512,512]{1,0:T(8,128)S(1)}, f32[192,512]{1,0:T...) custom-call(s32[1]{0:T(128)S(6)} %copy.13.sizes, ...), custom_call_target="tpu_custom_call" | custom-call | tf_op jit(solution)/shard_map/block_step/pallas_call | solution.py:466
  62.7 1.5 %finish.1 = (f32[64,256]{1,0:T(8,128)}, f32[64,256]{1,0:T(8,128)}, f32[64,512]{1,0:T(8,128)}, f32[128,512]{1,0:T(8,128)}, f32[192,512]{1,0:T(8,128)}) custom-call(f32[64,256]{1,0:T(8,128)S(1)} %get-tuple-element.18.diag, f32[64,256]{1,0:T(8,128)S(1)} %get-tuple-element.19.off, f32[64,512]{1,0:T(8,128)S(1)} %get-tuple-element.20.cross, ...), custom_call_target="tpu_custom_call" | custom-call | tf_op jit(solution)/shard_map/finish/pallas_call | solution.py:517

commit v5 on v4

--- a/solution.py
+++ b/solution.py
@@ -280,13 +280,24 @@
     hear(4, 2)
     hear(5, 2)
 
-    def part(q):
-        return pl.ds(al(16 * q, 16), 16)
-
-    for k in range(1, PLANE):
-        t, q, _ = plane_peer(k, 1)
-        remote(panel.at[part(q)], came_a.at[p], reduce_sem.at[0], reduce_sem.at[1], (t, ti)).start()
-    came_a[p] = panel[part(p), :]
+    jz = z // 2
+    steps = [lax.rem(jz + step, 8) for step in COMES]
+    places = [(8 * (j // 4), al(128 * (j % 4), 128)) for j in steps]
+
+    def tile_at(first, at):
+        row, col = places[at]
+        return pl.ds(al(first + row, 8), 8), pl.ds(col, 128)
+
+    waves = ((range(EARLY, 8), 1), (range(EARLY), 5))
+    for slots, sem in waves:
+        for k in range(1, PLANE):
+            t, q, _ = plane_peer(k, 1)
+            for at in slots:
+                src = panel.at[tile_at(16 * q, at)]
+                remote(src, came_a.at[p, at], reduce_sem.at[0], reduce_sem.at[sem], (t, ti)).start()
+    for at in range(8):
+        rows, cols = tile_at(16 * p, at)
+        came_a[p, at] = panel[rows, cols]
 
     local_pair.wait()
     mate_pair.wait_recv()
@@ -299,22 +310,24 @@
     u = dot_nt(hot, near[...]).astype(BF)
     wide[pl.ds(0, 128), :] = first_step(dot(u, xh[...]) + dot(u, xl[...]))
 
+    for slots, sem in waves:
+        count = len(slots)
+        span = pl.ds(slots[0], count)
+        drain(came_a.at[pl.ds(0, PLANE - 1), span], reduce_sem.at[sem])
+        total = came_a[0, span]
+        for q in range(1, PLANE):
+            total = total + came_a[q, span]
+        piece[span] = total
+        for at in sorted(slots, key=lambda at: -min(COMES[at], 8 - COMES[at])):
+            for one in range(2):
+                to = 2 * steps[at] + one
+                if at == 0:
+                    to = z + 1 - 2 * lax.rem(z, 2)
+                if at or one:
+                    device = (to * PLANE + p, ti)
+                    remote(piece.at[at], came_z.at[z], reduce_sem.at[2], reduce_sem.at[3], device).start()
+    came_z[z] = piece[0]
     others_a = came_a.at[pl.ds(0, PLANE - 1)]
-    drain(others_a, reduce_sem.at[1])
-    total = came_a[0]
-    for q in range(1, PLANE):
-        total = total + came_a[q]
-    piece[...] = total
-
-    def tile_of(first, j):
-        return pl.ds(al(first + 8 * (j // 4), 8), 8), pl.ds(al(128 * (j % 4), 128), 128)
-
-    for k in sorted(range(1, z_count), key=lambda k: -min(k, z_count - k)):
-        j = lax.rem(z + k, z_count) // 2
-        remote(piece.at[tile_of(0, j)], came_z.at[z], reduce_sem.at[2], reduce_sem.at[3], z_device(k)).start()
-    jz = z // 2
-    tile_rows, tile_cols = tile_of(0, jz)
-    came_z[z] = piece[tile_rows, tile_cols]
     cross_s = copy(start_hbm.at[:, near_cols], start_f.at[my_start, near_cols], cross, 4)
     mate_s = copy(start_hbm, start_f.at[my_start], mate, 4)
 
@@ -337,7 +350,7 @@
     total = came_z[0]
     for q in range(1, z_count):
         total = total + came_z[q]
-    tile_rows, tile_cols = tile_of(16 * p, jz)
+    tile_rows, tile_cols = tile_at(16 * p, 0)
     own_piece = PLANE * ti + p
     tiles[own_piece, 0] = total + base[tile_rows, tile_cols]
     for k in sorted(range(2, z_count, 2), key=lambda k: -min(k, z_count - k)):
@@ -358,7 +371,7 @@
             made = remote(here, here, reduce_sem.at[6], recv_p.at[16 * wave + k], plane_device(k))
             made.start()
             came.append((k, made))
-        remote(here, here, reduce_sem.at[7], reduce_sem.at[8], mate).start()
+        remote(here, here, reduce_sem.at[7], reduce_sem.at[8 + 3 * wave], mate).start()
         return came
 
     def hand_over(came, wave):
@@ -366,7 +379,7 @@
             made.wait_recv()
             _, q, hh = plane_peer(k, -1)
             ref = piece_of(hh, c, q, wave)
-            remote(ref, ref, reduce_sem.at[7], reduce_sem.at[8], mate).start()
+            remote(ref, ref, reduce_sem.at[7], reduce_sem.at[8 + 3 * wave], mate).start()
 
     v = wide[...]
     w = product(product(v, kh[...], kl[...]), xh[...], xl[...])
@@ -386,15 +399,12 @@
     s_high[...], s_low[...] = split(start_f[...])
     w_out[...] = product(yg, s_high[...], s_low[...])
 
-    places = [lax.rem(jz + step, 8) for step in COMES]
-    places = [(8 * (j // 4), al(128 * (j % 4), 128)) for j in places]
-
     def lay_out(cc, slots):
         def body(i, carry):
             q = PLANE * (2 * (i // PLANE) + cc) + lax.rem(i, PLANE)
             for at in slots:
-                row, col = places[at]
-                schur[pl.ds(al(16 * q + row, 8), 8), pl.ds(col, 128)] = tiles[q, at]
+                rows, cols = tile_at(16 * q, at)
+                schur[rows, cols] = tiles[q, at]
             return carry
 
         lax.fori_loop(0, 2 * PLANE, body, 0)
@@ -410,8 +420,10 @@
     cross_out[...] += nxt_came[:, pl.ds(256, 512)] * last
     others_p = schur.at[pl.ds(0, 16 * (2 * PLANE - 1))]
     everything = schur.at[pl.ds(0, 32 * PLANE)]
-    drain(everything, reduce_sem.at[8])
-    lay_out(1 - c, range(8))
+    drain(tiles.at[pl.ds(0, 2 * PLANE), pl.ds(0, EARLY)], reduce_sem.at[8])
+    lay_out(1 - c, range(EARLY))
+    drain(tiles.at[pl.ds(0, 2 * PLANE), pl.ds(EARLY, 8 - EARLY)], reduce_sem.at[11])
+    lay_out(1 - c, range(EARLY, 8))
 
     for group in range(4):
         drain(rows_x.at[pl.ds(0, 256)], send_sem.at[group])
@@ -486,8 +498,8 @@
             pltpu.VMEM((1, 512), jnp.int32),
             pltpu.VMEM((128, 512), F32),
             pltpu.VMEM((128, 512), F32),
-            pltpu.VMEM((PLANE, 16, 512), F32),
-            pltpu.VMEM((16, 512), F32),
+            pltpu.VMEM((PLANE, 8, 8, 128), F32),
+            pltpu.VMEM((8, 8, 128), F32),
             pltpu.VMEM((z_count, 8, 128), F32),
             pltpu.VMEM((4 * PLANE, 8, 8, 128), F32),
             pltpu.VMEM((order, 512), BF),
@@ -500,7 +512,7 @@
             DMA((6,)),
             DMA((22,)),
             DMA((4 * PLANE,)),
-            DMA((11,)),
+            DMA((12,)),
             pltpu.SemaphoreType.REGULAR((6,)),
         ],
         compiler_params=pltpu.CompilerParams(collective_id=0, has_side_effects=True, vmem_limit_bytes=GRANT),

time: 64.5 us -> 63.2 us (0.980)
  Pallas kernels: 62.9 us -> 61.6 us
    pallas_call x1, Pallas kernels: 61.4 us -> 60.1 us  [shards(): pl.pallas_call(functools.partial(block_kernel, z_count), out_shape=[pltpu...]
where the time goes in v5:
time: 63.2 us; the launch traced here: 63.1 us
  Pallas kernels  61.6 us (97%)
  between operations  1.45 us (2%)
    pallas_call x1, Pallas kernels, shards(): pl.pallas_call(functools.partial(block_kernel, z_count), out_shape=[pltpu...  60.1 us
    pallas_call x1, Pallas kernels, shards(): pl.pallas_call(finish_kernel, out_shape=[jax.ShapeDtypeStruct((64, 256),...  1.54 us

profile of v5, /device:TPU:1, one launch (start us, length us, event | category | flops | bytes accessed | tf_op | source)
XLA Modules:
  0.0 63.1 jit_solution(3547598829325231580)
XLA Ops:
  1.3 60.1 %block_step.1 = (f32[64,256]{1,0:T(8,128)S(1)}, f32[64,256]{1,0:T(8,128)S(1)}, f32[64,512]{1,0:T(8,128)S(1)}, f32[512,512]{1,0:T(8,128)S(1)}, f32[192,512]{1,0:T...) custom-call(s32[1]{0:T(128)S(6)} %copy.13.sizes, ...), custom_call_target="tpu_custom_call" | custom-call | tf_op jit(solution)/shard_map/block_step/pallas_call | solution.py:478
  61.4 1.5 %finish.1 = (f32[64,256]{1,0:T(8,128)}, f32[64,256]{1,0:T(8,128)}, f32[64,512]{1,0:T(8,128)}, f32[128,512]{1,0:T(8,128)}, f32[192,512]{1,0:T(8,128)}) custom-call(f32[64,256]{1,0:T(8,128)S(1)} %get-tuple-element.18.diag, f32[64,256]{1,0:T(8,128)S(1)} %get-tuple-element.19.off, f32[64,512]{1,0:T(8,128)S(1)} %get-tuple-element.20.cross, ...), custom_call_target="tpu_custom_call" | custom-call | tf_op jit(solution)/shard_map/finish/pallas_call | solution.py:529

commit v6 on v5

--- a/solution.py
+++ b/solution.py
@@ -262,6 +262,9 @@
     w_own = product(v, kh[:, pl.ds(0, HALF)], kl[:, pl.ds(0, HALF)])
     first, second = pl.ds(0, HALF), pl.ds(HALF, HALF)
     w_far = product(v[:, :HALF], kh[first, second], kl[first, second])
+    for i in range(2):
+        at = al(256 * h + 128 * i, 128)
+        g_perm[:, pl.ds(at, 128)] = permute(at).astype(BF)
     for made, ref in zip(cross_k, pieces(diag_k)):
         hand_on(made, ref, 3, pass_k)
     drain(rows_x.at[pl.ds(0, 64)], recv_t.at[pass_k])
@@ -271,8 +274,9 @@
     pass_g_rest = hand_on(cross_g_rest, rows_g.at[far, far_cols])
     w = product(product(v, kh[...], kl[...]), xh[...], xl[...])
     pass_g_rest.wait_recv()
-    for group in range(4):
-        g_perm[:, pl.ds(128 * group, 128)] = permute(128 * group).astype(BF)
+    for i in range(2):
+        at = al(256 - 256 * h + 128 * i, 128)
+        g_perm[:, pl.ds(at, 128)] = permute(at).astype(BF)
     y_high, y_low = split(2.0 * v - first_step(w))
     pass_pair = hand_on(cross_pair, pair.at[far])
     panel[...] = dot(y_high, g_perm[...]) + dot(y_low, g_perm[...])
@@ -343,7 +347,8 @@
     diag_out[...] = to_near[64:128, 256:512]
     cross_out[...] = to_glob[64:128, :]
     local_base.wait()
-    wide[...] = first_step(xh[mine, :].astype(F32) + xl[mine, :].astype(F32))
+    own_x = xh[mine, :].astype(F32) + xl[mine, :].astype(F32)
+    wide[...] = product(own_x, kh[...], kl[...])
 
     others_z = came_z.at[pl.ds(0, z_count - 1)]
     drain(others_z, reduce_sem.at[3])
@@ -381,7 +386,8 @@
             ref = piece_of(hh, c, q, wave)
             remote(ref, ref, reduce_sem.at[7], reduce_sem.at[8 + 3 * wave], mate).start()
 
-    v = wide[...]
+    own_x = xh[mine, :].astype(F32) + xl[mine, :].astype(F32)
+    v = 2.0 * own_x - product(wide[...], xh[...], xl[...])
     w = product(product(v, kh[...], kl[...]), xh[...], xl[...])
     drain(came_z.at[pl.ds(0, EARLY - 1)], reduce_sem.at[9])
     first_wave = spread(0)

time: 63.2 us -> 63.5 us (level)
  no operation moved by 1% of the time
where the time goes in v6:
time: 63.5 us; the launch traced here: 63.4 us
  Pallas kernels  62 us (98%)
  between operations  1.45 us (2%)
    pallas_call x1, Pallas kernels, shards(): pl.pallas_call(functools.partial(block_kernel, z_count), out_shape=[pltpu...  60.4 us
    pallas_call x1, Pallas kernels, shards(): pl.pallas_call(finish_kernel, out_shape=[jax.ShapeDtypeStruct((64, 256),...  1.54 us

profile of v6, /device:TPU:1, one launch (start us, length us, event | category | flops | bytes accessed | tf_op | source)
XLA Modules:
  0.0 63.4 jit_solution(17156652006008790889)
XLA Ops:
  1.3 60.4 %block_step.1 = (f32[64,256]{1,0:T(8,128)S(1)}, f32[64,256]{1,0:T(8,128)S(1)}, f32[64,512]{1,0:T(8,128)S(1)}, f32[512,512]{1,0:T(8,128)S(1)}, f32[192,512]{1,0:T...) custom-call(s32[1]{0:T(128)S(6)} %copy.13.sizes, ...), custom_call_target="tpu_custom_call" | custom-call | tf_op jit(solution)/shard_map/block_step/pallas_call | solution.py:484
  61.7 1.5 %finish.1 = (f32[64,256]{1,0:T(8,128)}, f32[64,256]{1,0:T(8,128)}, f32[64,512]{1,0:T(8,128)}, f32[128,512]{1,0:T(8,128)}, f32[192,512]{1,0:T(8,128)}) custom-call(f32[64,256]{1,0:T(8,128)S(1)} %get-tuple-element.18.diag, f32[64,256]{1,0:T(8,128)S(1)} %get-tuple-element.19.off, f32[64,512]{1,0:T(8,128)S(1)} %get-tuple-element.20.cross, ...), custom_call_target="tpu_custom_call" | custom-call | tf_op jit(solution)/shard_map/finish/pallas_call | solution.py:535

commit v7 on v6

--- a/solution.py
+++ b/solution.py
@@ -294,7 +294,7 @@
 
     waves = ((range(EARLY, 8), 1), (range(EARLY), 5))
     for slots, sem in waves:
-        for k in range(1, PLANE):
+        for k in (4, 3, 5, 2, 6, 1, 7):
             t, q, _ = plane_peer(k, 1)
             for at in slots:
                 src = panel.at[tile_at(16 * q, at)]
@@ -347,8 +347,7 @@
     diag_out[...] = to_near[64:128, 256:512]
     cross_out[...] = to_glob[64:128, :]
     local_base.wait()
-    own_x = xh[mine, :].astype(F32) + xl[mine, :].astype(F32)
-    wide[...] = product(own_x, kh[...], kl[...])
+    wide[...] = first_step(xh[mine, :].astype(F32) + xl[mine, :].astype(F32))
 
     others_z = came_z.at[pl.ds(0, z_count - 1)]
     drain(others_z, reduce_sem.at[3])
@@ -367,7 +366,7 @@
     def piece_of(hh, cc, q, wave):
         return tiles.at[PLANE * (2 * hh + cc) + q, pl.ds(0, EARLY) if wave == 0 else pl.ds(EARLY, 8 - EARLY)]
 
-    order = (9, 10, 11, 12, 13, 14, 15, 2, 3, 4, 5, 6, 1, 7, 8)
+    order = (12, 11, 13, 10, 14, 4, 9, 15, 3, 5, 2, 6, 8, 1, 7)
 
     def spread(wave):
         here = piece_of(h, c, p, wave)
@@ -386,8 +385,7 @@
             ref = piece_of(hh, c, q, wave)
             remote(ref, ref, reduce_sem.at[7], reduce_sem.at[8 + 3 * wave], mate).start()
 
-    own_x = xh[mine, :].astype(F32) + xl[mine, :].astype(F32)
-    v = 2.0 * own_x - product(wide[...], xh[...], xl[...])
+    v = wide[...]
     w = product(product(v, kh[...], kl[...]), xh[...], xl[...])
     drain(came_z.at[pl.ds(0, EARLY - 1)], reduce_sem.at[9])
     first_wave = spread(0)

time: 63.5 us -> 63 us (level)
  no operation moved by 1% of the time
where the time goes in v7:
time: 63 us; the launch traced here: 62.9 us
  Pallas kernels  61.5 us (98%)
  between operations  1.45 us (2%)
    pallas_call x1, Pallas kernels, shards(): pl.pallas_call(functools.partial(block_kernel, z_count), out_shape=[pltpu...  59.9 us
    pallas_call x1, Pallas kernels, shards(): pl.pallas_call(finish_kernel, out_shape=[jax.ShapeDtypeStruct((64, 256),...  1.54 us

profile of v7, /device:TPU:1, one launch (start us, length us, event | category | flops | bytes accessed | tf_op | source)
XLA Modules:
  0.0 62.9 jit_solution(14300810836585461008)
XLA Ops:
  1.3 59.9 %block_step.1 = (f32[64,256]{1,0:T(8,128)S(1)}, f32[64,256]{1,0:T(8,128)S(1)}, f32[64,512]{1,0:T(8,128)S(1)}, f32[512,512]{1,0:T(8,128)S(1)}, f32[192,512]{1,0:T...) custom-call(s32[1]{0:T(128)S(6)} %copy.13.sizes, ...), custom_call_target="tpu_custom_call" | custom-call | tf_op jit(solution)/shard_map/block_step/pallas_call | solution.py:482
  61.2 1.5 %finish.1 = (f32[64,256]{1,0:T(8,128)}, f32[64,256]{1,0:T(8,128)}, f32[64,512]{1,0:T(8,128)}, f32[128,512]{1,0:T(8,128)}, f32[192,512]{1,0:T(8,128)}) custom-call(f32[64,256]{1,0:T(8,128)S(1)} %get-tuple-element.18.diag, f32[64,256]{1,0:T(8,128)S(1)} %get-tuple-element.19.off, f32[64,512]{1,0:T(8,128)S(1)} %get-tuple-element.20.cross, ...), custom_call_target="tpu_custom_call" | custom-call | tf_op jit(solution)/shard_map/finish/pallas_call | solution.py:533
